TPU v7x, 256 devices: a whole 4x4x8 slice. The times are simulated.
256 devices in a mesh: frames: 32 (over y, z), codes: 8 (over x, core).
Axes of the slice: x: 4, y: 4, z: 8, core: 2. Of those that a mesh axis runs over, the one named last changes fastest.
Arguments:
- frames: bfloat16 [262144, 256], P(('frames', 'codes')), may hold values from -32 to 32
- codes: bfloat16 [65536, 256], P('codes'), may hold values from -2 to 2
- pattern: int32 [2048, 48], P('frames'), may hold values from 0 to 512, as said below
Outputs:
- row_potential: float32 [262144], P('frames')
- col_potential: float32 [65536], P('codes')
Inputs may be any that keep to these rules, and one draw needn't show every extreme that they name: `pattern`: each row lists distinct code blocks in increasing order, padded at its end with 512; it lists at least one block, and at most 6 of the 64 blocks k*64 to (k+1)*64 - 1 of any group k, exactly 6 in some row; every code block is listed by some row.
All inputs are finite; a program needn't handle non-finite values.
Results may differ from a plain program's by a relative error of at most 0.0046.
Values may be sent and summed in bfloat16 or wider, within the bound.
No kernel may reach another device: no remote copies, remote signals or barrier semaphores. Data moves between devices by JAX's collectives and lax.ppermute only.
A program may use at most 128 MiB of HBM per device.

v0:
```python
import functools
import math

import jax
import jax.numpy as jnp
from jax import lax
from jax.experimental import pallas as pl
from jax.experimental.pallas import tpu as pltpu
from jax.sharding import Mesh
from jax.sharding import PartitionSpec as P


BLK = 128
GB = 64
CAP = 6
ITERS = 3
PER = 8
CODES = ("codes_0", "codes_1")
FRAMES = ("frames_0", "frames_1")
FRAMES_CODES = ("frames_0", "frames_1", "codes_0", "codes_1")

NEG_FILL = -1e30
NEG_ROW = -1e29
SMALL = 1e-26
VMEM = 14 * 1024 * 1024


def tiles_kernel(picks, chunk, frames_ref, codes_ref, *refs):
    exp_ref, logit_ref, high_ref, lse_ref = refs[-4:]
    for b in range(PER):
        block = frames_ref[b * BLK : (b + 1) * BLK, :] * jnp.bfloat16(2.0)
        first = picks[(chunk[0] * PER + b) * 8]
        filled = []
        top = None
        for s in range(CAP):
            pick = picks[(chunk[0] * PER + b) * 8 + s]
            chosen = codes_ref[jnp.maximum(jnp.where(pick >= 0, pick, first), 0)]
            filled.append(jnp.where(pick >= 0, 1.0, 0.0))
            tile = lax.dot_general(
                chosen, block, (((1,), (1,)), ((), ())), preferred_element_type=jnp.float32
            )
            logit_ref[b, s * BLK : (s + 1) * BLK, :] = tile.astype(jnp.bfloat16)
            part = jnp.max(tile.reshape(BLK // 8, 8, BLK), axis=0)
            top = part if top is None else jnp.maximum(top, part)
        high = jnp.max(top, axis=0, keepdims=True).astype(jnp.bfloat16).astype(jnp.float32)
        total = None
        for s in range(CAP):
            tile = logit_ref[b, s * BLK : (s + 1) * BLK, :].astype(jnp.float32)
            terms = jnp.exp(tile - high)
            exp_ref[b, s * BLK : (s + 1) * BLK, :] = terms.astype(jnp.bfloat16)
            part = jnp.sum(terms.reshape(BLK // 8, 8, BLK), axis=0) * filled[s]
            total = part if total is None else total + part
        total = jnp.sum(total, axis=0, keepdims=True)
        high_ref[b : b + 1, :] = jnp.where(first >= 0, high, NEG_ROW)
        lse_ref[b : b + 1, :] = jnp.where(first >= 0, high + jnp.log(total), NEG_FILL)


def make_tiles(picks, chunk, frames, codes, chunks, before):
    tile_rows = CAP * BLK
    tiles = pl.BlockSpec((PER, tile_rows, BLK), lambda g, _, chunk: (chunk[0], 0, 0))
    lines = pl.BlockSpec((PER, BLK), lambda g, _, chunk: (chunk[0], 0))
    tiles_shape = jax.ShapeDtypeStruct((chunks * PER, tile_rows, BLK), jnp.bfloat16)
    lines_shape = jax.ShapeDtypeStruct((chunks * PER, BLK), jnp.float32)
    return pl.pallas_call(
        tiles_kernel,
        grid_spec=pltpu.PrefetchScalarGridSpec(
            num_scalar_prefetch=2,
            grid=(1,),
            in_specs=[
                pl.BlockSpec(frames.shape, lambda g, *_: (0, 0), pipeline_mode=pl.Buffered(1)),
                pl.BlockSpec(codes.shape, lambda g, *_: (0, 0, 0), pipeline_mode=pl.Buffered(1)),
                *[pl.BlockSpec(memory_space=pl.ANY) for _ in before],
            ],
            out_specs=[tiles, tiles, lines, lines],
        ),
        out_shape=[tiles_shape, tiles_shape, lines_shape, lines_shape],
        input_output_aliases={4 + k: k for k in range(len(before))},
        cost_estimate=pl.CostEstimate(
            flops=2 * tile_rows * PER * BLK * frames.shape[1],
            bytes_accessed=4 * tile_rows * PER * BLK,
            transcendentals=tile_rows * PER * BLK,
        ),
        compiler_params=pltpu.CompilerParams(vmem_limit_bytes=VMEM),
        name="make_tiles",
    )(picks, chunk, frames, codes, *before)


def pair(tiles_ref, q):
    return jnp.concatenate([tiles_ref[2 * q], tiles_ref[2 * q + 1]], axis=1)


def log_sum(pieces_ref):
    count = pieces_ref.shape[0]
    high = pieces_ref[0]
    for k in range(1, count):
        high = jnp.maximum(high, pieces_ref[k])
    total = jnp.exp(pieces_ref[0] - high)
    for k in range(1, count):
        total = total + jnp.exp(pieces_ref[k] - high)
    return high + jnp.log(total)


def split_dot(selector, values):
    upper = values.astype(jnp.bfloat16)
    lower = (values - upper.astype(jnp.float32)).astype(jnp.bfloat16)
    return jnp.dot(selector, upper, preferred_element_type=jnp.float32) + jnp.dot(
        selector, lower, preferred_element_type=jnp.float32
    )


def stable_pass(picks, logit_ref, shift_ref, out_ref, block_ref, high_ref, total_ref, by_code):
    high_ref[...] = jnp.full_like(high_ref, NEG_FILL)
    total_ref[...] = jnp.zeros_like(total_ref)

    def one_group(g, _):
        pltpu.sync_copy(logit_ref.at[pl.ds(g * PER, PER)], block_ref)

        def one_tile(index, _):
            b = index // CAP
            s = index - b * CAP
            row = g * PER + b
            pick = picks[row * 8 + s]

            @pl.when(pick >= 0)
            def _():
                rows = pl.ds(pl.multiple_of(s * BLK, BLK), BLK)
                tile = block_ref[b, rows, :].astype(jnp.float32)
                if by_code:
                    tile = jnp.transpose(tile + shift_ref[pl.ds(row, 1), :])
                    at = pl.ds(pick, 1)
                else:
                    shift = jnp.broadcast_to(shift_ref[pl.ds(pick, 1), :], (BLK, BLK))
                    tile = tile + jnp.transpose(shift)
                    at = pl.ds(row, 1)
                before = high_ref[at, :]
                high = jnp.maximum(before, jnp.max(tile, axis=0, keepdims=True))
                total_ref[at, :] = total_ref[at, :] * jnp.exp(before - high) + jnp.sum(
                    jnp.exp(tile - high), axis=0, keepdims=True
                )
                high_ref[at, :] = high

            return 0

        lax.fori_loop(0, CAP * PER, one_tile, 0)
        return 0

    lax.fori_loop(0, logit_ref.shape[0] // PER, one_group, 0)
    total = total_ref[...]
    out_ref[...] = jnp.where(
        total > 0.0, high_ref[...] + jnp.log(jnp.maximum(total, 1e-37)), NEG_FILL
    )


def column_kernel(
    copies, picks, pieces_ref, high_ref, picks_ref, exp_ref, logit_ref, row_ref, out_ref,
    scale_ref, sums_ref, peak_ref, lse_ref, block_ref, top_ref, total_ref,
):
    group = pl.program_id(0)

    @pl.when(group == 0)
    def _():
        row = -log_sum(pieces_ref)
        row_ref[...] = row
        weight = high_ref[...] + row
        peak = jnp.max(weight)
        peak_ref[0] = peak
        scale_ref[...] = jnp.exp(weight - peak)

    scale = scale_ref[pl.ds(pl.multiple_of(group * PER, PER), PER), :]
    wide = jnp.concatenate([scale] * PER, axis=1)
    lane_block = lax.broadcasted_iota(jnp.int32, wide.shape, 1) // BLK
    row_block = lax.broadcasted_iota(jnp.int32, wide.shape, 0)
    wide = jnp.where(lane_block == row_block, wide, 0.0).astype(jnp.bfloat16)
    sums = None
    for q in range(PER // 2):
        part = lax.dot_general(
            wide[:, 2 * q * BLK : 2 * (q + 1) * BLK],
            pair(exp_ref, q),
            (((1,), (1,)), ((), ())),
            preferred_element_type=jnp.float32,
        )
        sums = part if sums is None else sums + part
    sums_ref[pl.ds(pl.multiple_of(group * PER, PER), PER), :] = sums

    @pl.when(group == pl.num_programs(0) - 1)
    def _():
        blocks = lax.broadcasted_iota(jnp.int32, (GB, picks_ref.shape[1]), 0)
        total = jnp.zeros(lse_ref.shape, jnp.float32)
        used = jnp.zeros((GB, 1), jnp.float32)
        for s in range(CAP):
            hit = (picks_ref[s : s + 1, :] == blocks).astype(jnp.float32)
            used = used + jnp.sum(hit, axis=1, keepdims=True)
            total = total + split_dot(
                hit.astype(jnp.bfloat16), sums_ref[:, s * BLK : (s + 1) * BLK]
            )
        lse_ref[...] = jnp.where(
            total > 0.0, peak_ref[0] + jnp.log(jnp.maximum(total, 1e-37)), NEG_FILL
        )
        low = jnp.min(jnp.where(used > 0.0, total, 1.0))

        @pl.when(jnp.logical_not(low >= SMALL))
        def _():
            stable_pass(
                picks, logit_ref, row_ref, lse_ref, block_ref, top_ref, total_ref, True
            )

        for k in range(copies):
            out_ref[k] = lse_ref[...]


def row_kernel(
    copies, log_ratio, picks, pieces_ref, high_ref, picks_ref, exp_ref, logit_ref, out_ref,
    col_ref, scale_ref, sums_ref, peak_ref, lse_ref, block_ref, top_ref, total_ref,
):
    group = pl.program_id(0)

    @pl.when(group == 0)
    def _():
        col = log_ratio - log_sum(pieces_ref)
        col_ref[...] = col
        peak = jnp.max(col)
        peak_ref[0] = peak
        scale = jnp.exp(col - peak).astype(jnp.bfloat16)
        blocks = lax.broadcasted_iota(jnp.int32, (picks_ref.shape[0], GB), 1)
        for s in range(CAP):
            hit = (picks_ref[:, s : s + 1] == blocks).astype(jnp.float32).astype(jnp.bfloat16)
            scale_ref[:, s * BLK : (s + 1) * BLK] = jnp.dot(
                hit, scale, preferred_element_type=jnp.float32
            )

    at = pl.ds(pl.multiple_of(group * PER, PER), PER)
    scale = scale_ref[at, :].astype(jnp.bfloat16)
    row_block = lax.broadcasted_iota(jnp.int32, (PER, BLK), 0)
    total = jnp.zeros((PER, BLK), jnp.float32)
    for q in range(PER // 2):
        wide = jnp.dot(scale, pair(exp_ref, q), preferred_element_type=jnp.float32)
        total = total + jnp.where(row_block == 2 * q, wide[:, :BLK], 0.0)
        total = total + jnp.where(row_block == 2 * q + 1, wide[:, BLK:], 0.0)
    sums_ref[at, :] = total

    @pl.when(group == pl.num_programs(0) - 1)
    def _():
        total = sums_ref[...]
        lse_ref[...] = jnp.where(
            total > 0.0,
            high_ref[...] + (peak_ref[0] + jnp.log(jnp.maximum(total, 1e-37))),
            NEG_FILL,
        )
        low = jnp.min(jnp.where(picks_ref[:, 0:1] >= 0, total, 1.0))

        @pl.when(jnp.logical_not(low >= SMALL))
        def _():
            stable_pass(
                picks, logit_ref, col_ref, lse_ref, block_ref, top_ref, total_ref, False
            )

        for k in range(copies):
            out_ref[k] = lse_ref[...]


def whole(array):
    zeros = (0,) * array.ndim
    return pl.BlockSpec(array.shape, lambda g, _: zeros, pipeline_mode=pl.Buffered(1))


def column_pass(picks, pieces, high, picks_t, exps, logits, copies):
    groups = exps.shape[0] // PER
    rows = high.shape[0]
    return pl.pallas_call(
        functools.partial(column_kernel, copies),
        grid_spec=pltpu.PrefetchScalarGridSpec(
            num_scalar_prefetch=1,
            grid=(groups,),
            in_specs=[
                whole(pieces),
                whole(high),
                whole(picks_t),
                pl.BlockSpec((PER, *exps.shape[1:]), lambda g, _: (g, 0, 0)),
                pl.BlockSpec(memory_space=pl.ANY),
            ],
            out_specs=[
                pl.BlockSpec((rows, BLK), lambda g, _: (0, 0)),
                pl.BlockSpec((copies, GB, BLK), lambda g, _: (0, 0, 0)),
            ],
            scratch_shapes=[
                pltpu.VMEM((rows, BLK), jnp.float32),
                pltpu.VMEM((rows, CAP * BLK), jnp.float32),
                pltpu.SMEM((1,), jnp.float32),
                pltpu.VMEM((GB, BLK), jnp.float32),
                pltpu.VMEM((PER, *exps.shape[1:]), jnp.bfloat16),
                pltpu.VMEM((GB, BLK), jnp.float32),
                pltpu.VMEM((GB, BLK), jnp.float32),
            ],
        ),
        out_shape=[
            jax.ShapeDtypeStruct((rows, BLK), jnp.float32),
            jax.ShapeDtypeStruct((copies, GB, BLK), jnp.float32),
        ],
        compiler_params=pltpu.CompilerParams(vmem_limit_bytes=VMEM),
        name="column_pass",
    )(picks, pieces, high, picks_t, exps, logits)


def row_pass(picks, pieces, high, picks_v, exps, logits, copies, log_ratio):
    groups = exps.shape[0] // PER
    rows = high.shape[0]
    return pl.pallas_call(
        functools.partial(row_kernel, copies, log_ratio),
        grid_spec=pltpu.PrefetchScalarGridSpec(
            num_scalar_prefetch=1,
            grid=(groups,),
            in_specs=[
                whole(pieces),
                whole(high),
                whole(picks_v),
                pl.BlockSpec((PER, *exps.shape[1:]), lambda g, _: (g, 0, 0)),
                pl.BlockSpec(memory_space=pl.ANY),
            ],
            out_specs=pl.BlockSpec((copies, rows, BLK), lambda g, _: (0, 0, 0)),
            scratch_shapes=[
                pltpu.VMEM((GB, BLK), jnp.float32),
                pltpu.VMEM((rows, CAP * BLK), jnp.float32),
                pltpu.VMEM((rows, BLK), jnp.float32),
                pltpu.SMEM((1,), jnp.float32),
                pltpu.VMEM((rows, BLK), jnp.float32),
                pltpu.VMEM((PER, *exps.shape[1:]), jnp.bfloat16),
                pltpu.VMEM((rows, BLK), jnp.float32),
                pltpu.VMEM((rows, BLK), jnp.float32),
            ],
        ),
        out_shape=jax.ShapeDtypeStruct((copies, rows, BLK), jnp.float32),
        compiler_params=pltpu.CompilerParams(vmem_limit_bytes=VMEM),
        name="row_pass",
    )(picks, pieces, high, picks_v, exps, logits)


def candidates(pattern, low_block):
    _, slots = pattern.shape
    first = jnp.sum((pattern < low_block).astype(jnp.int32), axis=1)
    position = first[:, None] + jnp.arange(8, dtype=jnp.int32)[None, :]
    here = position[:, :, None] == jnp.arange(slots, dtype=jnp.int32)[None, None, :]
    offset = pattern - low_block
    found = jnp.max(jnp.where(here, offset[:, None, :], -1), axis=2)
    fits = (found < GB) & (jnp.arange(8, dtype=jnp.int32)[None, :] < CAP)
    return jnp.where(fits, found, -1)


def ring_shift(array, axis, step):
    size = lax.axis_size(axis)
    return lax.ppermute(array, axis, [(k, (k + step) % size) for k in range(size)])


def combine_kernel(offset, sign, pieces_ref, out_ref):
    lse = pieces_ref[0] if pieces_ref.shape[0] == 1 else log_sum(pieces_ref)
    lse = offset + sign * lse
    for k in range(out_ref.shape[0]):
        out_ref[k] = lse


def combine(pieces, copies, offset=0.0, sign=1.0):
    return pl.pallas_call(
        functools.partial(combine_kernel, offset, sign),
        out_shape=jax.ShapeDtypeStruct((copies, *pieces.shape[1:]), jnp.float32),
        compiler_params=pltpu.CompilerParams(vmem_limit_bytes=VMEM),
        name="combine",
    )(pieces)


def shards(frames, codes, pattern):
    along, core = CODES
    chips, cores = lax.axis_size(along), lax.axis_size(core)
    chip, half = lax.axis_index(along), lax.axis_index(core)
    code_copies = chips * cores
    steps = ((0,), (1, chips - 1), (2,))
    came = {0: frames, 1: ring_shift(frames, along, 1), chips - 1: ring_shift(frames, along, -1)}
    feature_width = codes.shape[1]
    num_blocks = codes.shape[0] // BLK
    frame_count = pattern.shape[0]
    picked = candidates(pattern, lax.axis_index(CODES) * num_blocks)
    codes = codes.reshape(num_blocks, BLK, feature_width)
    places = {
        (k, mine): (((chip - k) % chips) * cores + (half + mine) % cores).reshape(1)
        for step in steps
        for k in step
        for mine in (0, 1)
    }
    picks, picked, picked_t, places = lax.optimization_barrier(
        (picked.reshape(-1), picked, picked.T, places)
    )
    frames_total = frame_count * BLK * lax.axis_size(FRAMES)
    codes_total = num_blocks * BLK * lax.axis_size(CODES)
    log_ratio = math.log(frames_total / codes_total)
    made = ()
    for step in steps:
        blocks = tuple(came[k] for k in step)
        if made:
            blocks, made = lax.optimization_barrier((blocks, made))
        other = tuple(ring_shift(block, core, 1) for block in blocks)
        for mine, group in enumerate((blocks, other)):
            for k, block in zip(step, group):
                made = make_tiles(picks, places[k, mine], block, codes, code_copies, made)
                if 2 not in came:
                    far, made = lax.optimization_barrier((frames, made))
                    came[2] = ring_shift(far, along, 2)
    exps, logits, high, lse = made
    first, second = FRAMES
    pieces = combine(lse[None], code_copies)
    for iteration in range(ITERS):
        pieces = lax.all_to_all(pieces, CODES, 0, 0, tiled=True)
        row_potential, pieces = column_pass(
            picks, pieces, high, picked_t, exps, logits, lax.axis_size(first)
        )
        pieces = lax.all_to_all(pieces, first, 0, 0, tiled=True)
        pieces = combine(pieces, lax.axis_size(second))
        pieces = lax.all_to_all(pieces, second, 0, 0, tiled=True)
        if iteration < ITERS - 1:
            pieces = row_pass(
                picks, pieces, high, picked, exps, logits, code_copies, log_ratio
            )
    col_potential = combine(pieces, 1, log_ratio, -1.0)
    return (row_potential.reshape(-1), col_potential.reshape(-1))


def solution(mesh):
    torus = Mesh(mesh.devices.reshape(4, 8, 4, 2), ("frames_0", "frames_1", "codes_0", "codes_1"))
    placed = (P(FRAMES_CODES, None), P(CODES, None), P(FRAMES, None))

    return jax.shard_map(
        shards, mesh=torus, in_specs=placed, out_specs=(P(FRAMES), P(CODES)), check_vma=False
    )
```

profile of v0, /device:TPU:34, one launch (start us, length us, event | category | flops | bytes accessed | tf_op | source)
XLA Modules:
  0.0 369.1 jit_solution(7823633919837553464)
XLA Ops:
  0.7 1.6 collective-permute-start.1
  2.3 0.5 collective-permute-start.2
  2.8 0.8 convert_reduce_fusion
  4.2 2.2 copy-done
  6.4 1.0 copy-done.1
  7.4 2.1 make_tiles.8
  9.5 2.1 make_tiles.9
  11.6 3.6 collective-permute-done.1.frames_ref
  15.3 1.2 collective-permute-done.2.frames_ref
  17.0 2.3 collective-permute-start
  19.3 2.1 make_tiles.10
  21.4 2.1 make_tiles.11
  23.5 2.1 make_tiles.12
  25.6 2.1 make_tiles.13
  27.7 4.6 %collective-permute-done.frames_ref = bf16[1024,256]{1,0:T(8,128)(2,1)S(1)} collective-permute-done((bf16[1024,256]{1,0:T(8,128)(2,1)S(1)}, bf16[1024,256]{1,0:T(8,128)(2,1)S(1)}, u32[]{:S(2)}, u32[]{:S(2)}) %collective-permute-start) | collective-permute-done | bytes 524320 | tf_op jit(solution)/shard_map/ppermute | solution.py:350
  32.3 2.1 make_tiles.14
  34.4 2.1 make_tiles.15
  36.6 10.7 %all_to_all.45.pieces_ref = f32[8,64,128]{2,1,0:T(8,128)S(1)} all-to-all(f32[8,64,128]{2,1,0:T(8,128)S(1)} %combine.5), channel_id=1, replica_groups=mesh['frames_0'=4,'frames_1'=8,'codes_0'=4,'codes_1'=2] {'codes_0','code..., dimensions={0} | all-to-all | bytes 524288 | tf_op jit(solution)/shard_map/all_to_all | solution.py:409
  47.3 5.9 %column_pass.3 = (f32[64,128]{1,0:T(8,128)}, f32[4,64,128]{2,1,0:T(8,128)S(1)}) custom-call(s32[512]{0:T(512)S(1)} %and_select_fusion.1.picks, f32[8,64,128]{2,1,0:T(8,128)S(1)} %all_to_all.45.pieces_ref, f32[64,128]{1,0:T(8,128)S(1)} %get-tuple-element.119.high_ref, s32[8,64]{1,0:T(8,128)S(1)} %bitcast_select_fusion.picks_ref, ...), custom_call_target="tpu_custom_call" | custom-call | tf_op jit(solution)/shard_map/column_pass/pallas_call | solution.py:269
  53.2 10.2 %all_to_all.46.pieces_ref = f32[4,64,128]{2,1,0:T(8,128)S(1)} all-to-all(f32[4,64,128]{2,1,0:T(8,128)S(1)} %get-tuple-element.123), channel_id=1, replica_groups=mesh['frames_0'=4,'frames_1'=8,'codes_0'=4,'codes_1'=2] {'frames_0'}, dimensions={0} | all-to-all | bytes 262144 | tf_op jit(solution)/shard_map/all_to_all | solution.py:413
  63.5 17.4 %all_to_all.47.pieces_ref = f32[8,64,128]{2,1,0:T(8,128)S(1)} all-to-all(f32[8,64,128]{2,1,0:T(8,128)S(1)} %combine.6), channel_id=1, replica_groups=mesh['frames_0'=4,'frames_1'=8,'codes_0'=4,'codes_1'=2] {'frames_1'}, dimensions={0} | all-to-all | bytes 524288 | tf_op jit(solution)/shard_map/all_to_all | solution.py:415
  80.9 3.7 row_pass.2
  84.6 87.6 %all_to_all.48.pieces_ref = f32[8,64,128]{2,1,0:T(8,128)S(1)} all-to-all(f32[8,64,128]{2,1,0:T(8,128)S(1)} %row_pass.2), channel_id=1, replica_groups=mesh['frames_0'=4,'frames_1'=8,'codes_0'=4,'codes_1'=2] {'codes_0','code..., dimensions={0} | all-to-all | bytes 524288 | tf_op jit(solution)/shard_map/all_to_all | solution.py:409
  172.2 5.9 %column_pass.4 = (f32[64,128]{1,0:T(8,128)}, f32[4,64,128]{2,1,0:T(8,128)S(1)}) custom-call(s32[512]{0:T(512)S(1)} %and_select_fusion.1.picks, f32[8,64,128]{2,1,0:T(8,128)S(1)} %all_to_all.48.pieces_ref, f32[64,128]{1,0:T(8,128)S(1)} %get-tuple-element.119.high_ref, s32[8,64]{1,0:T(8,128)S(1)} %bitcast_select_fusion.picks_ref, ...), custom_call_target="tpu_custom_call" | custom-call | tf_op jit(solution)/shard_map/column_pass/pallas_call | solution.py:269
  178.1 9.7 %all_to_all.49.pieces_ref = f32[4,64,128]{2,1,0:T(8,128)S(1)} all-to-all(f32[4,64,128]{2,1,0:T(8,128)S(1)} %get-tuple-element.125), channel_id=1, replica_groups=mesh['frames_0'=4,'frames_1'=8,'codes_0'=4,'codes_1'=2] {'frames_0'}, dimensions={0} | all-to-all | bytes 262144 | tf_op jit(solution)/shard_map/all_to_all | solution.py:413
  187.8 13.9 %all_to_all.50.pieces_ref = f32[8,64,128]{2,1,0:T(8,128)S(1)} all-to-all(f32[8,64,128]{2,1,0:T(8,128)S(1)} %combine.7), channel_id=1, replica_groups=mesh['frames_0'=4,'frames_1'=8,'codes_0'=4,'codes_1'=2] {'frames_1'}, dimensions={0} | all-to-all | bytes 524288 | tf_op jit(solution)/shard_map/all_to_all | solution.py:415
  201.7 3.7 row_pass.3
  205.4 90.2 %all_to_all.51.pieces_ref = f32[8,64,128]{2,1,0:T(8,128)S(1)} all-to-all(f32[8,64,128]{2,1,0:T(8,128)S(1)} %row_pass.3), channel_id=1, replica_groups=mesh['frames_0'=4,'frames_1'=8,'codes_0'=4,'codes_1'=2] {'codes_0','code..., dimensions={0} | all-to-all | bytes 524288 | tf_op jit(solution)/shard_map/all_to_all | solution.py:409
  295.6 5.9 %column_pass.5 = (f32[64,128]{1,0:T(8,128)}, f32[4,64,128]{2,1,0:T(8,128)S(1)}) custom-call(s32[512]{0:T(512)S(1)} %and_select_fusion.1.picks, f32[8,64,128]{2,1,0:T(8,128)S(1)} %all_to_all.51.pieces_ref, f32[64,128]{1,0:T(8,128)S(1)} %get-tuple-element.119.high_ref, s32[8,64]{1,0:T(8,128)S(1)} %bitcast_select_fusion.picks_ref, ...), custom_call_target="tpu_custom_call" | custom-call | tf_op jit(solution)/shard_map/column_pass/pallas_call | solution.py:269
  301.5 46.7 %all_to_all.52.pieces_ref = f32[4,64,128]{2,1,0:T(8,128)S(1)} all-to-all(f32[4,64,128]{2,1,0:T(8,128)S(1)} %get-tuple-element.127), channel_id=1, replica_groups=mesh['frames_0'=4,'frames_1'=8,'codes_0'=4,'codes_1'=2] {'frames_0'}, dimensions={0} | all-to-all | bytes 262144 | tf_op jit(solution)/shard_map/all_to_all | solution.py:413
  348.2 20.2 %all_to_all.53.pieces_ref = f32[8,64,128]{2,1,0:T(8,128)S(1)} all-to-all(f32[8,64,128]{2,1,0:T(8,128)S(1)} %combine.8), channel_id=1, replica_groups=mesh['frames_0'=4,'frames_1'=8,'codes_0'=4,'codes_1'=2] {'frames_1'}, dimensions={0} | all-to-all | bytes 524288 | tf_op jit(solution)/shard_map/all_to_all | solution.py:415
  368.5 0.7 combine.9
  (28 shorter events, 1.3 us)
Async XLA Ops:
  0.6 8.9 %collective-permute-start.3 = (bf16[1024,256]{1,0:T(8,128)(2,1)}, bf16[1024,256]{1,0:T(8,128)(2,1)S(1)}, u32[]{:S(2)}, u32[]{:S(2)}) collective-permute-start(bf16[1024,256]{1,0:T(8,128)(2,1)} %frames_ref.1), channel_id=1, source_target_pairs={{0,1},{1,0},{2,3},{3,2},{4,5},{5,4},{6,7},{7,6},{8,9},{9,8},{10,11... | collective-permute-start | bytes 1572872 | tf_op jit(solution)/shard_map/ppermute | solution.py:350
  0.7 14.5 %collective-permute-start.1 = (bf16[1024,256]{1,0:T(8,128)(2,1)}, bf16[1024,256]{1,0:T(8,128)(2,1)S(1)}, u32[]{:S(2)}, u32[]{:S(2)}) collective-permute-start(bf16[1024,256]{1,0:T(8,128)(2,1)} %frames_ref.1), channel_id=1, source_target_pairs={{0,2},{2,4},{4,6},{6,0},{1,3},{3,5},{5,7},{7,1},{8,10},{10,12},{12... | collective-permute-start | bytes 1572872 | tf_op jit(solution)/shard_map/ppermute | solution.py:350
  2.3 14.2 %collective-permute-start.2 = (bf16[1024,256]{1,0:T(8,128)(2,1)}, bf16[1024,256]{1,0:T(8,128)(2,1)S(1)}, u32[]{:S(2)}, u32[]{:S(2)}) collective-permute-start(bf16[1024,256]{1,0:T(8,128)(2,1)} %frames_ref.1), channel_id=1, source_target_pairs={{0,6},{2,0},{4,2},{6,4},{1,7},{3,1},{5,3},{7,5},{8,14},{10,8},{12,... | collective-permute-start | bytes 1572872 | tf_op jit(solution)/shard_map/ppermute | solution.py:350
  4.2 2.2 copy-start
  6.4 1.0 copy-start.1
  9.5 7.5 %copy-start.2 = (bf16[1024,256]{1,0:T(8,128)(2,1)S(1)}, bf16[1024,256]{1,0:T(8,128)(2,1)}, u32[]{:S(2)}) copy-start(bf16[1024,256]{1,0:T(8,128)(2,1)} %frames_ref.1) | copy-start | bytes 1572868
  16.5 7.0 %collective-permute-start.5 = (bf16[1024,256]{1,0:T(8,128)(2,1)S(1)}, bf16[1024,256]{1,0:T(8,128)(2,1)S(1)}, u32[]{:S(2)}, u32[]{:S(2)}) collective-permute-start(bf16[1024,256]{1,0:T(8,128)(2,1)S(1)} %collective-permute-done.1.frames_ref), channel_id=1, source_target_pairs={{0,1},{1,0},{2,3},{3,2},{4,5},{5,4},{6,7},{7,6},{8,9},{9,8},{10,11... | collective-permute-start | bytes 1572872 | tf_op jit(solution)/shard_map/ppermute | solution.py:350
  16.5 9.2 %collective-permute-start.4 = (bf16[1024,256]{1,0:T(8,128)(2,1)S(1)}, bf16[1024,256]{1,0:T(8,128)(2,1)S(1)}, u32[]{:S(2)}, u32[]{:S(2)}) collective-permute-start(bf16[1024,256]{1,0:T(8,128)(2,1)S(1)} %collective-permute-done.2.frames_ref), channel_id=1, source_target_pairs={{0,1},{1,0},{2,3},{3,2},{4,5},{5,4},{6,7},{7,6},{8,9},{9,8},{10,11... | collective-permute-start | bytes 1572872 | tf_op jit(solution)/shard_map/ppermute | solution.py:350
  17.0 15.3 %collective-permute-start = (bf16[1024,256]{1,0:T(8,128)(2,1)S(1)}, bf16[1024,256]{1,0:T(8,128)(2,1)S(1)}, u32[]{:S(2)}, u32[]{:S(2)}) collective-permute-start(bf16[1024,256]{1,0:T(8,128)(2,1)S(1)} %copy-done.2), channel_id=1, source_target_pairs={{0,4},{2,6},{4,0},{6,2},{1,5},{3,7},{5,1},{7,3},{8,12},{10,14},{12... | collective-permute-start | bytes 1572872 | tf_op jit(solution)/shard_map/ppermute | solution.py:350
  32.3 2.1 collective-permute-start.6
where the time goes:
time: 371 us; the launch traced here: 369 us
  blocking collectives  307 us (83%)
  Pallas kernels  42.7 us (12%)
  waiting for transfers between devices  9.46 us (3%)
  starting transfers between devices  5.03 us (1%)
    all_to_all x3, blocking collectives, shards(): pieces = lax.all_to_all(pieces, CODES, 0, 0, tiled=True)  189 us
    all_to_all x3, blocking collectives, shards(): pieces = lax.all_to_all(pieces, first, 0, 0, tiled=True)  66.6 us
    all_to_all x3, blocking collectives, shards(): pieces = lax.all_to_all(pieces, second, 0, 0, tiled=True)  51.5 us
    pallas_call x3, Pallas kernels, column_pass(): pl.pallas_call(functools.partial(column_kernel, copies), grid_spec=pltpu....  17.7 us
    pallas_call x8, Pallas kernels, make_tiles(): pl.pallas_call(tiles_kernel, grid_spec=pltpu.PrefetchScalarGridSpec(num_s...  16.8 us
    ppermute x7, waiting for transfers between devices, ring_shift(): lax.ppermute(array, axis, [(k, (k + step) % size) for k in range(size)])  9.46 us
  transfers between devices with their start and end apart: 7, of which 3 were waited for; matrix products, arithmetic and copies ran while one was open for 0% of the time, Pallas kernels for 4%

commit v1 on v0

--- a/solution.py
+++ b/solution.py
@@ -25,10 +25,12 @@
 VMEM = 14 * 1024 * 1024
 
 
-def tiles_kernel(picks, chunk, frames_ref, codes_ref, *refs):
+def tiles_kernel(parts, picks, chunk, codes_ref, *refs):
     exp_ref, logit_ref, high_ref, lse_ref = refs[-4:]
     for b in range(PER):
-        block = frames_ref[b * BLK : (b + 1) * BLK, :] * jnp.bfloat16(2.0)
+        held = PER // parts
+        at = (b % held) * BLK
+        block = refs[b // held][at : at + BLK, :] * jnp.bfloat16(2.0)
         first = picks[(chunk[0] * PER + b) * 8]
         filled = []
         top = None
@@ -56,48 +58,90 @@
 
 
 def make_tiles(picks, chunk, frames, codes, chunks, before):
+    parts = len(frames)
     tile_rows = CAP * BLK
     tiles = pl.BlockSpec((PER, tile_rows, BLK), lambda g, _, chunk: (chunk[0], 0, 0))
     lines = pl.BlockSpec((PER, BLK), lambda g, _, chunk: (chunk[0], 0))
     tiles_shape = jax.ShapeDtypeStruct((chunks * PER, tile_rows, BLK), jnp.bfloat16)
     lines_shape = jax.ShapeDtypeStruct((chunks * PER, BLK), jnp.float32)
     return pl.pallas_call(
-        tiles_kernel,
+        functools.partial(tiles_kernel, parts),
         grid_spec=pltpu.PrefetchScalarGridSpec(
             num_scalar_prefetch=2,
             grid=(1,),
             in_specs=[
-                pl.BlockSpec(frames.shape, lambda g, *_: (0, 0), pipeline_mode=pl.Buffered(1)),
                 pl.BlockSpec(codes.shape, lambda g, *_: (0, 0, 0), pipeline_mode=pl.Buffered(1)),
+                *[
+                    pl.BlockSpec(part.shape, lambda g, *_: (0, 0), pipeline_mode=pl.Buffered(1))
+                    for part in frames
+                ],
                 *[pl.BlockSpec(memory_space=pl.ANY) for _ in before],
             ],
             out_specs=[tiles, tiles, lines, lines],
         ),
         out_shape=[tiles_shape, tiles_shape, lines_shape, lines_shape],
-        input_output_aliases={4 + k: k for k in range(len(before))},
+        input_output_aliases={3 + parts + k: k for k in range(len(before))},
         cost_estimate=pl.CostEstimate(
-            flops=2 * tile_rows * PER * BLK * frames.shape[1],
+            flops=2 * tile_rows * PER * BLK * codes.shape[2],
             bytes_accessed=4 * tile_rows * PER * BLK,
             transcendentals=tile_rows * PER * BLK,
         ),
         compiler_params=pltpu.CompilerParams(vmem_limit_bytes=VMEM),
         name="make_tiles",
-    )(picks, chunk, frames, codes, *before)
+    )(picks, chunk, codes, *frames, *before)
+
+
+def halves_kernel(left_ref, right_ref, upper_ref, lower_ref):
+    half = upper_ref.shape[0]
+    upper_ref[...] = left_ref[:half, :]
+    lower_ref[...] = right_ref[half:, :]
+
+
+def halves(left, right):
+    shape = jax.ShapeDtypeStruct((left.shape[0] // 2, left.shape[1]), left.dtype)
+    return pl.pallas_call(
+        halves_kernel,
+        out_shape=[shape, shape],
+        compiler_params=pltpu.CompilerParams(vmem_limit_bytes=VMEM),
+        name="halves",
+    )(left, right)
 
 
 def pair(tiles_ref, q):
     return jnp.concatenate([tiles_ref[2 * q], tiles_ref[2 * q + 1]], axis=1)
 
 
-def log_sum(pieces_ref):
-    count = pieces_ref.shape[0]
-    high = pieces_ref[0]
-    for k in range(1, count):
-        high = jnp.maximum(high, pieces_ref[k])
-    total = jnp.exp(pieces_ref[0] - high)
-    for k in range(1, count):
-        total = total + jnp.exp(pieces_ref[k] - high)
+def log_sum(pieces):
+    high = pieces[0]
+    for piece in pieces[1:]:
+        high = jnp.maximum(high, piece)
+    total = jnp.exp(pieces[0] - high)
+    for piece in pieces[1:]:
+        total = total + jnp.exp(piece - high)
     return high + jnp.log(total)
+
+
+def arrived(refs, kept_ref=None):
+    if len(refs) == 1:
+        return [refs[0][k] for k in range(refs[0].shape[0])]
+    pieces = []
+    for k in range(refs[0].shape[0]):
+        pieces.append(refs[0][k] + refs[1][k].astype(jnp.float32))
+        if kept_ref is not None:
+            kept_ref[k] = pieces[k]
+    return pieces
+
+
+def send(piece, out_ref, own_ref=None, kept_ref=None):
+    if own_ref is None:
+        change = piece
+        if kept_ref is not None:
+            kept_ref[...] = piece
+    else:
+        change = (piece - own_ref[...]).astype(jnp.bfloat16)
+        kept_ref[...] = own_ref[...] + change.astype(jnp.float32)
+    for k in range(out_ref.shape[0]):
+        out_ref[k] = change
 
 
 def split_dot(selector, values):
@@ -151,15 +195,17 @@
     )
 
 
-def column_kernel(
-    copies, picks, pieces_ref, high_ref, picks_ref, exp_ref, logit_ref, row_ref, out_ref,
-    scale_ref, sums_ref, peak_ref, lse_ref, block_ref, top_ref, total_ref,
-):
+def column_kernel(pieces, picks, *refs):
+    piece_refs, (high_ref, picks_ref, exp_ref, logit_ref, row_ref, out_ref), refs = (
+        refs[:pieces], refs[pieces : pieces + 6], refs[pieces + 6 :]
+    )
+    kept_ref = refs[0] if pieces == 2 else None
+    scale_ref, sums_ref, peak_ref, lse_ref, block_ref, top_ref, total_ref = refs[-7:]
     group = pl.program_id(0)
 
     @pl.when(group == 0)
     def _():
-        row = -log_sum(pieces_ref)
+        row = -log_sum(arrived(piece_refs, kept_ref))
         row_ref[...] = row
         weight = high_ref[...] + row
         peak = jnp.max(weight)
@@ -204,19 +250,20 @@
                 picks, logit_ref, row_ref, lse_ref, block_ref, top_ref, total_ref, True
             )
 
-        for k in range(copies):
-            out_ref[k] = lse_ref[...]
-
-
-def row_kernel(
-    copies, log_ratio, picks, pieces_ref, high_ref, picks_ref, exp_ref, logit_ref, out_ref,
-    col_ref, scale_ref, sums_ref, peak_ref, lse_ref, block_ref, top_ref, total_ref,
-):
+        send(lse_ref[...], out_ref)
+
+
+def row_kernel(pieces, log_ratio, picks, *refs):
+    piece_refs, (own_ref, high_ref, picks_ref, exp_ref, logit_ref, out_ref, sent_ref), refs = (
+        refs[:pieces], refs[pieces : pieces + 7], refs[pieces + 7 :]
+    )
+    kept_ref = refs[0] if pieces == 2 else None
+    col_ref, scale_ref, sums_ref, peak_ref, lse_ref, block_ref, top_ref, total_ref = refs[-8:]
     group = pl.program_id(0)
 
     @pl.when(group == 0)
     def _():
-        col = log_ratio - log_sum(pieces_ref)
+        col = log_ratio - log_sum(arrived(piece_refs, kept_ref))
         col_ref[...] = col
         peak = jnp.max(col)
         peak_ref[0] = peak
@@ -254,8 +301,7 @@
                 picks, logit_ref, col_ref, lse_ref, block_ref, top_ref, total_ref, False
             )
 
-        for k in range(copies):
-            out_ref[k] = lse_ref[...]
+        send(lse_ref[...], out_ref, own_ref, sent_ref)
 
 
 def whole(array):
@@ -263,25 +309,33 @@
     return pl.BlockSpec(array.shape, lambda g, _: zeros, pipeline_mode=pl.Buffered(1))
 
 
+def fixed(shape):
+    zeros = (0,) * len(shape)
+    return pl.BlockSpec(shape, lambda g, _: zeros)
+
+
 def column_pass(picks, pieces, high, picks_t, exps, logits, copies):
     groups = exps.shape[0] // PER
     rows = high.shape[0]
+    kept = pieces[:1] if len(pieces) == 2 else ()
+    outs = [
+        jax.ShapeDtypeStruct((rows, BLK), jnp.float32),
+        jax.ShapeDtypeStruct((copies, GB, BLK), jnp.float32),
+        *[jax.ShapeDtypeStruct(piece.shape, piece.dtype) for piece in kept],
+    ]
     return pl.pallas_call(
-        functools.partial(column_kernel, copies),
+        functools.partial(column_kernel, len(pieces)),
         grid_spec=pltpu.PrefetchScalarGridSpec(
             num_scalar_prefetch=1,
             grid=(groups,),
             in_specs=[
-                whole(pieces),
+                *[whole(piece) for piece in pieces],
                 whole(high),
                 whole(picks_t),
                 pl.BlockSpec((PER, *exps.shape[1:]), lambda g, _: (g, 0, 0)),
                 pl.BlockSpec(memory_space=pl.ANY),
             ],
-            out_specs=[
-                pl.BlockSpec((rows, BLK), lambda g, _: (0, 0)),
-                pl.BlockSpec((copies, GB, BLK), lambda g, _: (0, 0, 0)),
-            ],
+            out_specs=[fixed(out.shape) for out in outs],
             scratch_shapes=[
                 pltpu.VMEM((rows, BLK), jnp.float32),
                 pltpu.VMEM((rows, CAP * BLK), jnp.float32),
@@ -292,31 +346,35 @@
                 pltpu.VMEM((GB, BLK), jnp.float32),
             ],
         ),
-        out_shape=[
-            jax.ShapeDtypeStruct((rows, BLK), jnp.float32),
-            jax.ShapeDtypeStruct((copies, GB, BLK), jnp.float32),
-        ],
+        out_shape=outs,
         compiler_params=pltpu.CompilerParams(vmem_limit_bytes=VMEM),
         name="column_pass",
-    )(picks, pieces, high, picks_t, exps, logits)
-
-
-def row_pass(picks, pieces, high, picks_v, exps, logits, copies, log_ratio):
+    )(picks, *pieces, high, picks_t, exps, logits)
+
+
+def row_pass(picks, pieces, own, high, picks_v, exps, logits, copies, log_ratio):
     groups = exps.shape[0] // PER
     rows = high.shape[0]
+    kept = pieces[:1] if len(pieces) == 2 else ()
+    outs = [
+        jax.ShapeDtypeStruct((copies, rows, BLK), jnp.bfloat16),
+        jax.ShapeDtypeStruct((rows, BLK), jnp.float32),
+        *[jax.ShapeDtypeStruct(piece.shape, piece.dtype) for piece in kept],
+    ]
     return pl.pallas_call(
-        functools.partial(row_kernel, copies, log_ratio),
+        functools.partial(row_kernel, len(pieces), log_ratio),
         grid_spec=pltpu.PrefetchScalarGridSpec(
             num_scalar_prefetch=1,
             grid=(groups,),
             in_specs=[
-                whole(pieces),
+                *[whole(piece) for piece in pieces],
+                whole(own),
                 whole(high),
                 whole(picks_v),
                 pl.BlockSpec((PER, *exps.shape[1:]), lambda g, _: (g, 0, 0)),
                 pl.BlockSpec(memory_space=pl.ANY),
             ],
-            out_specs=pl.BlockSpec((copies, rows, BLK), lambda g, _: (0, 0, 0)),
+            out_specs=[fixed(out.shape) for out in outs],
             scratch_shapes=[
                 pltpu.VMEM((GB, BLK), jnp.float32),
                 pltpu.VMEM((rows, CAP * BLK), jnp.float32),
@@ -328,10 +386,10 @@
                 pltpu.VMEM((rows, BLK), jnp.float32),
             ],
         ),
-        out_shape=jax.ShapeDtypeStruct((copies, rows, BLK), jnp.float32),
+        out_shape=outs,
         compiler_params=pltpu.CompilerParams(vmem_limit_bytes=VMEM),
         name="row_pass",
-    )(picks, pieces, high, picks_v, exps, logits)
+    )(picks, *pieces, own, high, picks_v, exps, logits)
 
 
 def candidates(pattern, low_block):
@@ -350,20 +408,29 @@
     return lax.ppermute(array, axis, [(k, (k + step) % size) for k in range(size)])
 
 
-def combine_kernel(offset, sign, pieces_ref, out_ref):
-    lse = pieces_ref[0] if pieces_ref.shape[0] == 1 else log_sum(pieces_ref)
-    lse = offset + sign * lse
-    for k in range(out_ref.shape[0]):
-        out_ref[k] = lse
-
-
-def combine(pieces, copies, offset=0.0, sign=1.0):
+def combine_kernel(counts, offset, sign, *refs):
+    pieces, olds = counts
+    lse = log_sum(arrived(refs[:pieces]))
+    old_refs, out_ref, kept_refs = (
+        refs[pieces : pieces + olds], refs[pieces + olds], refs[pieces + olds + 1 :]
+    )
+    own_ref, kept_ref = (*old_refs, None)[0], (*kept_refs, None)[0]
+    send(offset + sign * lse, out_ref, own_ref, kept_ref)
+
+
+def combine(pieces, copies, own=None, offset=0.0, sign=1.0):
+    lines = pieces[0].shape[1:]
+    olds = () if own is None else (own,)
+    kind = jnp.bfloat16 if olds else jnp.float32
     return pl.pallas_call(
-        functools.partial(combine_kernel, offset, sign),
-        out_shape=jax.ShapeDtypeStruct((copies, *pieces.shape[1:]), jnp.float32),
+        functools.partial(combine_kernel, (len(pieces), len(olds)), offset, sign),
+        out_shape=[
+            jax.ShapeDtypeStruct((copies, *lines), kind),
+            jax.ShapeDtypeStruct(lines, jnp.float32),
+        ],
         compiler_params=pltpu.CompilerParams(vmem_limit_bytes=VMEM),
         name="combine",
-    )(pieces)
+    )(*pieces, *olds)
 
 
 def shards(frames, codes, pattern):
@@ -371,8 +438,7 @@
     chips, cores = lax.axis_size(along), lax.axis_size(core)
     chip, half = lax.axis_index(along), lax.axis_index(core)
     code_copies = chips * cores
-    steps = ((0,), (1, chips - 1), (2,))
-    came = {0: frames, 1: ring_shift(frames, along, 1), chips - 1: ring_shift(frames, along, -1)}
+    from_left, from_right = ring_shift(frames, along, 1), ring_shift(frames, along, -1)
     feature_width = codes.shape[1]
     num_blocks = codes.shape[0] // BLK
     frame_count = pattern.shape[0]
@@ -380,8 +446,7 @@
     codes = codes.reshape(num_blocks, BLK, feature_width)
     places = {
         (k, mine): (((chip - k) % chips) * cores + (half + mine) % cores).reshape(1)
-        for step in steps
-        for k in step
+        for k in (0, 1, chips - 1, 2)
         for mine in (0, 1)
     }
     picks, picked, picked_t, places = lax.optimization_barrier(
@@ -391,33 +456,51 @@
     codes_total = num_blocks * BLK * lax.axis_size(CODES)
     log_ratio = math.log(frames_total / codes_total)
     made = ()
-    for step in steps:
-        blocks = tuple(came[k] for k in step)
-        if made:
-            blocks, made = lax.optimization_barrier((blocks, made))
-        other = tuple(ring_shift(block, core, 1) for block in blocks)
-        for mine, group in enumerate((blocks, other)):
-            for k, block in zip(step, group):
-                made = make_tiles(picks, places[k, mine], block, codes, code_copies, made)
-                if 2 not in came:
-                    far, made = lax.optimization_barrier((frames, made))
-                    came[2] = ring_shift(far, along, 2)
+
+    def use(made, k, mine, *parts):
+        return make_tiles(picks, places[k, mine], parts, codes, code_copies, made)
+
+    other = ring_shift(frames, core, 1)
+    made = use(made, 0, 0, frames)
+    made = use(made, 0, 1, other)
+    from_left, from_right, made = lax.optimization_barrier((from_left, from_right, made))
+    upper, lower = halves(from_left, from_right)
+    upper = ring_shift(upper, along, 1)
+    lower = ring_shift(lower, along, -1)
+    swapped = tuple(ring_shift(block, core, 1) for block in (from_left, from_right))
+    made = use(made, 1, 0, from_left)
+    made = use(made, chips - 1, 0, from_right)
+    made = use(made, 1, 1, swapped[0])
+    made = use(made, chips - 1, 1, swapped[1])
+    upper, lower, made = lax.optimization_barrier((upper, lower, made))
+    swapped = tuple(ring_shift(block, core, 1) for block in (upper, lower))
+    made = use(made, 2, 0, upper, lower)
+    made = use(made, 2, 1, *swapped)
     exps, logits, high, lse = made
     first, second = FRAMES
-    pieces = combine(lse[None], code_copies)
+
+    def exchange(pieces, axes):
+        return lax.all_to_all(pieces, axes, 0, 0, tiled=True)
+
+    pieces, row_sent = combine((lse[None],), code_copies)
+    rows = (exchange(pieces, CODES),)
+    cols = ()
+    col_sent = None
     for iteration in range(ITERS):
-        pieces = lax.all_to_all(pieces, CODES, 0, 0, tiled=True)
-        row_potential, pieces = column_pass(
-            picks, pieces, high, picked_t, exps, logits, lax.axis_size(first)
+        row_potential, pieces, *kept = column_pass(
+            picks, rows, high, picked_t, exps, logits, lax.axis_size(first)
         )
-        pieces = lax.all_to_all(pieces, first, 0, 0, tiled=True)
-        pieces = combine(pieces, lax.axis_size(second))
-        pieces = lax.all_to_all(pieces, second, 0, 0, tiled=True)
+        rows = tuple(kept) or rows
+        pieces = exchange(pieces, first)
+        pieces, col_sent = combine((pieces,), lax.axis_size(second), col_sent)
+        cols = (*cols[:1], exchange(pieces, second))
         if iteration < ITERS - 1:
-            pieces = row_pass(
-                picks, pieces, high, picked, exps, logits, code_copies, log_ratio
+            pieces, row_sent, *kept = row_pass(
+                picks, cols, row_sent, high, picked, exps, logits, code_copies, log_ratio
             )
-    col_potential = combine(pieces, 1, log_ratio, -1.0)
+            cols = tuple(kept) or cols
+            rows = (rows[0], exchange(pieces, CODES))
+    _, col_potential = combine(cols, 1, None, log_ratio, -1.0)
     return (row_potential.reshape(-1), col_potential.reshape(-1))
 
 

time: 371 us -> 362 us (0.976)
  blocking collectives: 307 us -> 300 us
  waiting for transfers between devices: 9.46 us -> 4.88 us
    all_to_all x9, blocking collectives: 307 us -> 300 us  [exchange(): return lax.all_to_all(pieces, axes, 0, 0, tiled=True)]
    ppermute x7 -> x9, waiting for transfers between devices: 9.46 us -> 4.88 us  [ring_shift(): lax.ppermute(array, axis, [(k, (k + step) % size) for k in range(size)])]
    pallas_call x18 -> x19, Pallas kernels: 42.7 us -> 44.1 us  [the longest x3 17.9 us: column_pass(): pl.pallas_call(functools.partial(column_kernel, len(pieces)), grid_spec=p...]
  transfers between devices with their start and end apart: 7 -> 9, of which waited for: 3 -> 2; matrix products, arithmetic and copies ran while one was open for 0% -> 0% of each run, Pallas kernels for 4% -> 4%
where the time goes in v1:
time: 362 us; the launch traced here: 359 us
  blocking collectives  300 us (83%)
  Pallas kernels  44.1 us (12%)
  starting transfers between devices  5.4 us (1%)
  waiting for transfers between devices  4.88 us (1%)
    all_to_all x9, blocking collectives, exchange(): return lax.all_to_all(pieces, axes, 0, 0, tiled=True)  300 us
    pallas_call x3, Pallas kernels, column_pass(): pl.pallas_call(functools.partial(column_kernel, len(pieces)), grid_spec=p...  17.9 us
    pallas_call x8, Pallas kernels, make_tiles(): pl.pallas_call(functools.partial(tiles_kernel, parts), grid_spec=pltpu.Pr...  16.7 us
    pallas_call x2, Pallas kernels, row_pass(): pl.pallas_call(functools.partial(row_kernel, len(pieces), log_ratio), gri...  7.98 us
  transfers between devices with their start and end apart: 9, of which 2 were waited for; matrix products, arithmetic and copies ran while one was open for 0% of the time, Pallas kernels for 4%

profile of v1, /device:TPU:34, one launch (start us, length us, event | category | flops | bytes accessed | tf_op | source)
XLA Modules:
  0.0 359.5 jit_solution(19177440202249609)
XLA Ops:
  0.7 1.6 collective-permute-start
  2.8 0.8 convert_reduce_fusion
  4.2 2.2 copy-done
  6.4 1.0 copy-done.2
  7.4 2.1 make_tiles.8
  9.5 2.1 make_tiles.9
  11.6 3.6 %collective-permute-done.left_ref.refs_0_ = bf16[1024,256]{1,0:T(8,128)(2,1)S(1)} collective-permute-done((bf16[1024,256]{1,0:T(8,128)(2,1)}, bf16[1024,256]{1,0:T(8,128)(2,1)S(1)}, u32[]{:S(2)}, u32[]{:S(2)}) %collective-permute-start) | collective-permute-done | bytes 524320 | tf_op jit(solution)/shard_map/ppermute | solution.py:408
  15.3 1.2 collective-permute-done.1.right_ref.refs_0_
  17.0 1.3 collective-permute-start.3
  18.3 0.8 collective-permute-start.4
  19.1 2.1 make_tiles.10
  21.2 2.1 make_tiles.11
  23.3 2.1 make_tiles.12
  25.4 2.1 make_tiles.13
  28.1 2.1 make_tiles.14
  30.3 2.1 make_tiles.15
  32.4 10.6 %all_to_all.45.refs_0_ = f32[8,64,128]{2,1,0:T(8,128)S(1)} all-to-all(f32[8,64,128]{2,1,0:T(8,128)S(1)} %get-tuple-element.128), channel_id=1, replica_groups=mesh['frames_0'=4,'frames_1'=8,'codes_0'=4,'codes_1'=2] {'codes_0','code..., dimensions={0} | all-to-all | bytes 524288 | tf_op jit(solution)/shard_map/all_to_all | solution.py:483
  43.0 5.9 %column_pass.3 = (f32[64,128]{1,0:T(8,128)}, f32[4,64,128]{2,1,0:T(8,128)S(1)}) custom-call(s32[512]{0:T(512)S(1)} %and_select_fusion.1.picks, f32[8,64,128]{2,1,0:T(8,128)S(1)} %all_to_all.45.refs_0_, f32[64,128]{1,0:T(8,128)S(1)} %get-tuple-element.129.refs_1_.refs_2_.refs_3_, s32[8,64]{1,0:T(8,128)S(1)} %bitcast_select_fusion.refs_2_.refs_3_, ...), custom_call_target="tpu_custom_call" | custom-call | tf_op jit(solution)/shard_map/column_pass/pallas_call | solution.py:326
  48.9 10.2 %all_to_all.46.refs_0_ = f32[4,64,128]{2,1,0:T(8,128)S(1)} all-to-all(f32[4,64,128]{2,1,0:T(8,128)S(1)} %get-tuple-element.133), channel_id=1, replica_groups=mesh['frames_0'=4,'frames_1'=8,'codes_0'=4,'codes_1'=2] {'frames_0'}, dimensions={0} | all-to-all | bytes 262144 | tf_op jit(solution)/shard_map/all_to_all | solution.py:483
  59.2 17.4 %all_to_all.47.refs_0_ = f32[8,64,128]{2,1,0:T(8,128)S(1)} all-to-all(f32[8,64,128]{2,1,0:T(8,128)S(1)} %get-tuple-element.134), channel_id=1, replica_groups=mesh['frames_0'=4,'frames_1'=8,'codes_0'=4,'codes_1'=2] {'frames_1'}, dimensions={0} | all-to-all | bytes 524288 | tf_op jit(solution)/shard_map/all_to_all | solution.py:483
  76.6 3.7 %row_pass.2 = (bf16[8,64,128]{2,1,0:T(8,128)(2,1)S(1)}, f32[64,128]{1,0:T(8,128)S(1)}) custom-call(s32[512]{0:T(512)S(1)} %and_select_fusion.1.picks, f32[8,64,128]{2,1,0:T(8,128)S(1)} %all_to_all.47.refs_0_, f32[64,128]{1,0:T(8,128)S(1)} %get-tuple-element.135.refs_1_, f32[64,128]{1,0:T(8,128)S(1)} %get-tuple-element.129.refs_1_.refs_2_.refs_3_, ...), custom_call_target="tpu_custom_call" | custom-call | tf_op jit(solution)/shard_map/row_pass/pallas_call | solution.py:364
  80.3 86.2 %all_to_all.48.refs_1_ = bf16[8,64,128]{2,1,0:T(8,128)(2,1)S(1)} all-to-all(bf16[8,64,128]{2,1,0:T(8,128)(2,1)S(1)} %get-tuple-element.137), channel_id=1, replica_groups=mesh['frames_0'=4,'frames_1'=8,'codes_0'=4,'codes_1'=2] {'codes_0','code..., dimensions={0} | all-to-all | bytes 262144 | tf_op jit(solution)/shard_map/all_to_all | solution.py:483
  166.5 5.9 %column_pass.4 = (f32[64,128]{1,0:T(8,128)}, f32[4,64,128]{2,1,0:T(8,128)S(1)}, f32[8,64,128]{2,1,0:T(8,128)S(1)}) custom-call(s32[512]{0:T(512)S(1)} %and_select_fusion.1.picks, f32[8,64,128]{2,1,0:T(8,128)S(1)} %all_to_all.45.refs_0_, bf16[8,64,128]{2,1,0:T(8,128)(2,1)S(1)} %all_to_all.48.refs_1_, ...), custom_call_target="tpu_custom_call" | custom-call | tf_op jit(solution)/shard_map/column_pass/pallas_call | solution.py:326
  172.5 9.7 %all_to_all.49.refs_0_ = f32[4,64,128]{2,1,0:T(8,128)S(1)} all-to-all(f32[4,64,128]{2,1,0:T(8,128)S(1)} %get-tuple-element.139), channel_id=1, replica_groups=mesh['frames_0'=4,'frames_1'=8,'codes_0'=4,'codes_1'=2] {'frames_0'}, dimensions={0} | all-to-all | bytes 262144 | tf_op jit(solution)/shard_map/all_to_all | solution.py:483
  182.2 12.5 %all_to_all.50.refs_1_ = bf16[8,64,128]{2,1,0:T(8,128)(2,1)S(1)} all-to-all(bf16[8,64,128]{2,1,0:T(8,128)(2,1)S(1)} %get-tuple-element.141), channel_id=1, replica_groups=mesh['frames_0'=4,'frames_1'=8,'codes_0'=4,'codes_1'=2] {'frames_1'}, dimensions={0} | all-to-all | bytes 262144 | tf_op jit(solution)/shard_map/all_to_all | solution.py:483
  194.7 4.3 %row_pass.3 = (bf16[8,64,128]{2,1,0:T(8,128)(2,1)S(1)}, f32[64,128]{1,0:T(8,128)}, f32[8,64,128]{2,1,0:T(8,128)S(1)}) custom-call(s32[512]{0:T(512)S(1)} %and_select_fusion.1.picks, f32[8,64,128]{2,1,0:T(8,128)S(1)} %all_to_all.47.refs_0_, bf16[8,64,128]{2,1,0:T(8,128)(2,1)S(1)} %all_to_all.50.refs_1_, f32[64,128]{1,0:T(8,128)S(1)} %get-tuple-element.142.refs_2_, ...), custom_call_target="tpu_custom_call" | custom-call | tf_op jit(solution)/shard_map/row_pass/pallas_call | solution.py:364
  199.0 89.0 %all_to_all.51.refs_1_ = bf16[8,64,128]{2,1,0:T(8,128)(2,1)S(1)} all-to-all(bf16[8,64,128]{2,1,0:T(8,128)(2,1)S(1)} %get-tuple-element.143), channel_id=1, replica_groups=mesh['frames_0'=4,'frames_1'=8,'codes_0'=4,'codes_1'=2] {'codes_0','code..., dimensions={0} | all-to-all | bytes 262144 | tf_op jit(solution)/shard_map/all_to_all | solution.py:483
  287.9 6.0 %column_pass.5 = (f32[64,128]{1,0:T(8,128)}, f32[4,64,128]{2,1,0:T(8,128)S(1)}, f32[8,64,128]{2,1,0:T(8,128)}) custom-call(s32[512]{0:T(512)S(1)} %and_select_fusion.1.picks, f32[8,64,128]{2,1,0:T(8,128)S(1)} %get-tuple-element.138.refs_0_, bf16[8,64,128]{2,1,0:T(8,128)(2,1)S(1)} %all_to_all.51.refs_1_, ...), custom_call_target="tpu_custom_call" | custom-call | tf_op jit(solution)/shard_map/column_pass/pallas_call | solution.py:326
  293.9 46.7 %all_to_all.52.refs_0_ = f32[4,64,128]{2,1,0:T(8,128)S(1)} all-to-all(f32[4,64,128]{2,1,0:T(8,128)S(1)} %get-tuple-element.146), channel_id=1, replica_groups=mesh['frames_0'=4,'frames_1'=8,'codes_0'=4,'codes_1'=2] {'frames_0'}, dimensions={0} | all-to-all | bytes 262144 | tf_op jit(solution)/shard_map/all_to_all | solution.py:483
  340.7 0.7 combine.8
  341.3 17.4 %all_to_all.53.refs_1_ = bf16[8,64,128]{2,1,0:T(8,128)(2,1)S(1)} all-to-all(bf16[8,64,128]{2,1,0:T(8,128)(2,1)S(1)} %get-tuple-element.148), channel_id=1, replica_groups=mesh['frames_0'=4,'frames_1'=8,'codes_0'=4,'codes_1'=2] {'frames_1'}, dimensions={0} | all-to-all | bytes 262144 | tf_op jit(solution)/shard_map/all_to_all | solution.py:483
  358.8 0.7 combine.9
  (33 shorter events, 2.5 us)
Async XLA Ops:
  0.6 8.9 %collective-permute-start.2 = (bf16[1024,256]{1,0:T(8,128)(2,1)}, bf16[1024,256]{1,0:T(8,128)(2,1)S(1)}, u32[]{:S(2)}, u32[]{:S(2)}) collective-permute-start(bf16[1024,256]{1,0:T(8,128)(2,1)} %refs_0_.1), channel_id=1, source_target_pairs={{0,1},{1,0},{2,3},{3,2},{4,5},{5,4},{6,7},{7,6},{8,9},{9,8},{10,11... | collective-permute-start | bytes 1572872 | tf_op jit(solution)/shard_map/ppermute | solution.py:408
  0.7 14.5 %collective-permute-start = (bf16[1024,256]{1,0:T(8,128)(2,1)}, bf16[1024,256]{1,0:T(8,128)(2,1)S(1)}, u32[]{:S(2)}, u32[]{:S(2)}) collective-permute-start(bf16[1024,256]{1,0:T(8,128)(2,1)} %refs_0_.1), channel_id=1, source_target_pairs={{0,2},{2,4},{4,6},{6,0},{1,3},{3,5},{5,7},{7,1},{8,10},{10,12},{12... | collective-permute-start | bytes 1572872 | tf_op jit(solution)/shard_map/ppermute | solution.py:408
  2.3 14.2 %collective-permute-start.1 = (bf16[1024,256]{1,0:T(8,128)(2,1)}, bf16[1024,256]{1,0:T(8,128)(2,1)S(1)}, u32[]{:S(2)}, u32[]{:S(2)}) collective-permute-start(bf16[1024,256]{1,0:T(8,128)(2,1)} %refs_0_.1), channel_id=1, source_target_pairs={{0,6},{2,0},{4,2},{6,4},{1,7},{3,1},{5,3},{7,5},{8,14},{10,8},{12,... | collective-permute-start | bytes 1572872 | tf_op jit(solution)/shard_map/ppermute | solution.py:408
  4.2 2.2 copy-start
  6.4 1.0 copy-start.2
  9.5 9.6 %copy-start.1 = (bf16[8192,256]{1,0:T(8,128)(2,1)S(1)}, bf16[8192,256]{1,0:T(8,128)(2,1)}, u32[]{:S(2)}) copy-start(bf16[8192,256]{1,0:T(8,128)(2,1)} %param.4) | copy-start | bytes 12582916
  16.5 6.8 %collective-permute-start.6 = (bf16[1024,256]{1,0:T(8,128)(2,1)S(1)}, bf16[1024,256]{1,0:T(8,128)(2,1)S(1)}, u32[]{:S(2)}, u32[]{:S(2)}) collective-permute-start(bf16[1024,256]{1,0:T(8,128)(2,1)S(1)} %collective-permute-done.left_ref.refs_0_), channel_id=1, source_target_pairs={{0,1},{1,0},{2,3},{3,2},{4,5},{5,4},{6,7},{7,6},{8,9},{9,8},{10,11... | collective-permute-start | bytes 1572872 | tf_op jit(solution)/shard_map/ppermute | solution.py:408
  16.5 8.9 %collective-permute-start.5 = (bf16[1024,256]{1,0:T(8,128)(2,1)S(1)}, bf16[1024,256]{1,0:T(8,128)(2,1)S(1)}, u32[]{:S(2)}, u32[]{:S(2)}) collective-permute-start(bf16[1024,256]{1,0:T(8,128)(2,1)S(1)} %collective-permute-done.1.right_ref.refs_0_), channel_id=1, source_target_pairs={{0,1},{1,0},{2,3},{3,2},{4,5},{5,4},{6,7},{7,6},{8,9},{9,8},{10,11... | collective-permute-start | bytes 1572872 | tf_op jit(solution)/shard_map/ppermute | solution.py:408
  17.0 10.5 %collective-permute-start.3 = (bf16[512,256]{1,0:T(8,128)(2,1)S(1)}, bf16[512,256]{1,0:T(8,128)(2,1)S(1)}, u32[]{:S(2)}, u32[]{:S(2)}) collective-permute-start(bf16[512,256]{1,0:T(8,128)(2,1)S(1)} %get-tuple-element.90), channel_id=1, source_target_pairs={{0,2},{2,4},{4,6},{6,0},{1,3},{3,5},{5,7},{7,1},{8,10},{10,12},{12... | collective-permute-start | bytes 786440 | tf_op jit(solution)/shard_map/ppermute | solution.py:408
  18.3 9.2 %collective-permute-start.4 = (bf16[512,256]{1,0:T(8,128)(2,1)S(1)}, bf16[512,256]{1,0:T(8,128)(2,1)S(1)}, u32[]{:S(2)}, u32[]{:S(2)}) collective-permute-start(bf16[512,256]{1,0:T(8,128)(2,1)S(1)} %get-tuple-element.91), channel_id=1, source_target_pairs={{0,6},{2,0},{4,2},{6,4},{1,7},{3,1},{5,3},{7,5},{8,14},{10,8},{12,... | collective-permute-start | bytes 786440 | tf_op jit(solution)/shard_map/ppermute | solution.py:408
  27.5 2.7 collective-permute-start.7
  27.6 2.6 collective-permute-start.8

commit v2 on v1

--- a/solution.py
+++ b/solution.py
@@ -15,6 +15,7 @@
 CAP = 6
 ITERS = 3
 PER = 8
+STEP = 4
 CODES = ("codes_0", "codes_1")
 FRAMES = ("frames_0", "frames_1")
 FRAMES_CODES = ("frames_0", "frames_1", "codes_0", "codes_1")
@@ -32,17 +33,21 @@
         at = (b % held) * BLK
         block = refs[b // held][at : at + BLK, :] * jnp.bfloat16(2.0)
         first = picks[(chunk[0] * PER + b) * 8]
-        filled = []
-        top = None
+        chosen, filled = [], []
         for s in range(CAP):
             pick = picks[(chunk[0] * PER + b) * 8 + s]
-            chosen = codes_ref[jnp.maximum(jnp.where(pick >= 0, pick, first), 0)]
+            chosen.append(codes_ref[jnp.maximum(jnp.where(pick >= 0, pick, first), 0)])
             filled.append(jnp.where(pick >= 0, 1.0, 0.0))
-            tile = lax.dot_general(
-                chosen, block, (((1,), (1,)), ((), ())), preferred_element_type=jnp.float32
-            )
-            logit_ref[b, s * BLK : (s + 1) * BLK, :] = tile.astype(jnp.bfloat16)
-            part = jnp.max(tile.reshape(BLK // 8, 8, BLK), axis=0)
+        top = None
+        for s in range(0, CAP, 3):
+            three = lax.dot_general(
+                jnp.concatenate(chosen[s : s + 3], axis=0),
+                block,
+                (((1,), (1,)), ((), ())),
+                preferred_element_type=jnp.float32,
+            )
+            logit_ref[b, s * BLK : (s + 3) * BLK, :] = three.astype(jnp.bfloat16)
+            part = jnp.max(three.reshape(3 * BLK // 8, 8, BLK), axis=0)
             top = part if top is None else jnp.maximum(top, part)
         high = jnp.max(top, axis=0, keepdims=True).astype(jnp.bfloat16).astype(jnp.float32)
         total = None
@@ -91,22 +96,6 @@
     )(picks, chunk, codes, *frames, *before)
 
 
-def halves_kernel(left_ref, right_ref, upper_ref, lower_ref):
-    half = upper_ref.shape[0]
-    upper_ref[...] = left_ref[:half, :]
-    lower_ref[...] = right_ref[half:, :]
-
-
-def halves(left, right):
-    shape = jax.ShapeDtypeStruct((left.shape[0] // 2, left.shape[1]), left.dtype)
-    return pl.pallas_call(
-        halves_kernel,
-        out_shape=[shape, shape],
-        compiler_params=pltpu.CompilerParams(vmem_limit_bytes=VMEM),
-        name="halves",
-    )(left, right)
-
-
 def pair(tiles_ref, q):
     return jnp.concatenate([tiles_ref[2 * q], tiles_ref[2 * q + 1]], axis=1)
 
@@ -139,7 +128,8 @@
             kept_ref[...] = piece
     else:
         change = (piece - own_ref[...]).astype(jnp.bfloat16)
-        kept_ref[...] = own_ref[...] + change.astype(jnp.float32)
+        if kept_ref is not None:
+            kept_ref[...] = own_ref[...] + change.astype(jnp.float32)
     for k in range(out_ref.shape[0]):
         out_ref[k] = change
 
@@ -195,12 +185,14 @@
     )
 
 
-def column_kernel(pieces, picks, *refs):
-    piece_refs, (high_ref, picks_ref, exp_ref, logit_ref, row_ref, out_ref), refs = (
-        refs[:pieces], refs[pieces : pieces + 6], refs[pieces + 6 :]
-    )
-    kept_ref = refs[0] if pieces == 2 else None
-    scale_ref, sums_ref, peak_ref, lse_ref, block_ref, top_ref, total_ref = refs[-7:]
+def column_kernel(pieces, last, picks, *refs):
+    piece_refs, (high_ref, picks_ref, exp_ref, logit_ref, out_ref), refs = (
+        refs[:pieces], refs[pieces : pieces + 5], refs[pieces + 5 :]
+    )
+    kept_ref = refs[0] if pieces == 2 and not last else None
+    row_ref, scale_ref, sums_ref, peak_ref, lse_ref, block_ref, top_ref, total_ref = refs[-8:]
+    if last:
+        row_ref = refs[0]
     group = pl.program_id(0)
 
     @pl.when(group == 0)
@@ -212,21 +204,22 @@
         peak_ref[0] = peak
         scale_ref[...] = jnp.exp(weight - peak)
 
-    scale = scale_ref[pl.ds(pl.multiple_of(group * PER, PER), PER), :]
-    wide = jnp.concatenate([scale] * PER, axis=1)
-    lane_block = lax.broadcasted_iota(jnp.int32, wide.shape, 1) // BLK
-    row_block = lax.broadcasted_iota(jnp.int32, wide.shape, 0)
-    wide = jnp.where(lane_block == row_block, wide, 0.0).astype(jnp.bfloat16)
-    sums = None
-    for q in range(PER // 2):
-        part = lax.dot_general(
-            wide[:, 2 * q * BLK : 2 * (q + 1) * BLK],
-            pair(exp_ref, q),
-            (((1,), (1,)), ((), ())),
-            preferred_element_type=jnp.float32,
-        )
-        sums = part if sums is None else sums + part
-    sums_ref[pl.ds(pl.multiple_of(group * PER, PER), PER), :] = sums
+    for part in range(STEP):
+        at = pl.ds(pl.multiple_of((group * STEP + part) * PER, PER), PER)
+        wide = jnp.concatenate([scale_ref[at, :]] * PER, axis=1)
+        lane_block = lax.broadcasted_iota(jnp.int32, wide.shape, 1) // BLK
+        row_block = lax.broadcasted_iota(jnp.int32, wide.shape, 0)
+        wide = jnp.where(lane_block == row_block, wide, 0.0).astype(jnp.bfloat16)
+        sums = None
+        for q in range(PER // 2):
+            product = lax.dot_general(
+                wide[:, 2 * q * BLK : 2 * (q + 1) * BLK],
+                pair(exp_ref, part * PER // 2 + q),
+                (((1,), (1,)), ((), ())),
+                preferred_element_type=jnp.float32,
+            )
+            sums = product if sums is None else sums + product
+        sums_ref[at, :] = sums
 
     @pl.when(group == pl.num_programs(0) - 1)
     def _():
@@ -253,11 +246,12 @@
         send(lse_ref[...], out_ref)
 
 
-def row_kernel(pieces, log_ratio, picks, *refs):
-    piece_refs, (own_ref, high_ref, picks_ref, exp_ref, logit_ref, out_ref, sent_ref), refs = (
-        refs[:pieces], refs[pieces : pieces + 7], refs[pieces + 7 :]
-    )
-    kept_ref = refs[0] if pieces == 2 else None
+def row_kernel(pieces, keep, log_ratio, picks, *refs):
+    piece_refs, (own_ref, high_ref, picks_ref, exp_ref, logit_ref, out_ref), refs = (
+        refs[:pieces], refs[pieces : pieces + 6], refs[pieces + 6 :]
+    )
+    sent_ref = refs[0] if keep else None
+    kept_ref = refs[keep] if pieces == 2 else None
     col_ref, scale_ref, sums_ref, peak_ref, lse_ref, block_ref, top_ref, total_ref = refs[-8:]
     group = pl.program_id(0)
 
@@ -275,15 +269,18 @@
                 hit, scale, preferred_element_type=jnp.float32
             )
 
-    at = pl.ds(pl.multiple_of(group * PER, PER), PER)
-    scale = scale_ref[at, :].astype(jnp.bfloat16)
-    row_block = lax.broadcasted_iota(jnp.int32, (PER, BLK), 0)
-    total = jnp.zeros((PER, BLK), jnp.float32)
-    for q in range(PER // 2):
-        wide = jnp.dot(scale, pair(exp_ref, q), preferred_element_type=jnp.float32)
-        total = total + jnp.where(row_block == 2 * q, wide[:, :BLK], 0.0)
-        total = total + jnp.where(row_block == 2 * q + 1, wide[:, BLK:], 0.0)
-    sums_ref[at, :] = total
+    for part in range(STEP):
+        at = pl.ds(pl.multiple_of((group * STEP + part) * PER, PER), PER)
+        scale = scale_ref[at, :].astype(jnp.bfloat16)
+        row_block = lax.broadcasted_iota(jnp.int32, (PER, BLK), 0)
+        total = jnp.zeros((PER, BLK), jnp.float32)
+        for q in range(PER // 2):
+            wide = jnp.dot(
+                scale, pair(exp_ref, part * PER // 2 + q), preferred_element_type=jnp.float32
+            )
+            total = total + jnp.where(row_block == 2 * q, wide[:, :BLK], 0.0)
+            total = total + jnp.where(row_block == 2 * q + 1, wide[:, BLK:], 0.0)
+        sums_ref[at, :] = total
 
     @pl.when(group == pl.num_programs(0) - 1)
     def _():
@@ -314,29 +311,31 @@
     return pl.BlockSpec(shape, lambda g, _: zeros)
 
 
-def column_pass(picks, pieces, high, picks_t, exps, logits, copies):
+def column_pass(picks, pieces, high, picks_t, exps, logits, copies, last):
     groups = exps.shape[0] // PER
     rows = high.shape[0]
     kept = pieces[:1] if len(pieces) == 2 else ()
+    if last:
+        kept = (high,)
     outs = [
-        jax.ShapeDtypeStruct((rows, BLK), jnp.float32),
         jax.ShapeDtypeStruct((copies, GB, BLK), jnp.float32),
         *[jax.ShapeDtypeStruct(piece.shape, piece.dtype) for piece in kept],
     ]
     return pl.pallas_call(
-        functools.partial(column_kernel, len(pieces)),
+        functools.partial(column_kernel, len(pieces), last),
         grid_spec=pltpu.PrefetchScalarGridSpec(
             num_scalar_prefetch=1,
-            grid=(groups,),
+            grid=(groups // STEP,),
             in_specs=[
                 *[whole(piece) for piece in pieces],
                 whole(high),
                 whole(picks_t),
-                pl.BlockSpec((PER, *exps.shape[1:]), lambda g, _: (g, 0, 0)),
+                pl.BlockSpec((STEP * PER, *exps.shape[1:]), lambda g, _: (g, 0, 0)),
                 pl.BlockSpec(memory_space=pl.ANY),
             ],
             out_specs=[fixed(out.shape) for out in outs],
             scratch_shapes=[
+                pltpu.VMEM((rows, BLK), jnp.float32),
                 pltpu.VMEM((rows, BLK), jnp.float32),
                 pltpu.VMEM((rows, CAP * BLK), jnp.float32),
                 pltpu.SMEM((1,), jnp.float32),
@@ -352,26 +351,26 @@
     )(picks, *pieces, high, picks_t, exps, logits)
 
 
-def row_pass(picks, pieces, own, high, picks_v, exps, logits, copies, log_ratio):
+def row_pass(picks, pieces, own, high, picks_v, exps, logits, copies, log_ratio, keep):
     groups = exps.shape[0] // PER
     rows = high.shape[0]
     kept = pieces[:1] if len(pieces) == 2 else ()
     outs = [
         jax.ShapeDtypeStruct((copies, rows, BLK), jnp.bfloat16),
-        jax.ShapeDtypeStruct((rows, BLK), jnp.float32),
+        *[jax.ShapeDtypeStruct((rows, BLK), jnp.float32) for _ in range(keep)],
         *[jax.ShapeDtypeStruct(piece.shape, piece.dtype) for piece in kept],
     ]
     return pl.pallas_call(
-        functools.partial(row_kernel, len(pieces), log_ratio),
+        functools.partial(row_kernel, len(pieces), keep, log_ratio),
         grid_spec=pltpu.PrefetchScalarGridSpec(
             num_scalar_prefetch=1,
-            grid=(groups,),
+            grid=(groups // STEP,),
             in_specs=[
                 *[whole(piece) for piece in pieces],
                 whole(own),
                 whole(high),
                 whole(picks_v),
-                pl.BlockSpec((PER, *exps.shape[1:]), lambda g, _: (g, 0, 0)),
+                pl.BlockSpec((STEP * PER, *exps.shape[1:]), lambda g, _: (g, 0, 0)),
                 pl.BlockSpec(memory_space=pl.ANY),
             ],
             out_specs=[fixed(out.shape) for out in outs],
@@ -408,25 +407,42 @@
     return lax.ppermute(array, axis, [(k, (k + step) % size) for k in range(size)])
 
 
-def combine_kernel(counts, offset, sign, *refs):
+def finish_kernel(log_ratio, kept_ref, change_ref, row_ref, row_out_ref, col_out_ref):
+    row_out_ref[...] = row_ref[...]
+    col_out_ref[...] = log_ratio - log_sum(arrived((kept_ref, change_ref)))
+
+
+def finish(cols, row, log_ratio):
+    return pl.pallas_call(
+        functools.partial(finish_kernel, log_ratio),
+        out_shape=[
+            jax.ShapeDtypeStruct(row.shape, jnp.float32),
+            jax.ShapeDtypeStruct(cols[0].shape[1:], jnp.float32),
+        ],
+        compiler_params=pltpu.CompilerParams(vmem_limit_bytes=VMEM),
+        name="finish",
+    )(*cols, row)
+
+
+def combine_kernel(counts, *refs):
     pieces, olds = counts
     lse = log_sum(arrived(refs[:pieces]))
     old_refs, out_ref, kept_refs = (
         refs[pieces : pieces + olds], refs[pieces + olds], refs[pieces + olds + 1 :]
     )
     own_ref, kept_ref = (*old_refs, None)[0], (*kept_refs, None)[0]
-    send(offset + sign * lse, out_ref, own_ref, kept_ref)
-
-
-def combine(pieces, copies, own=None, offset=0.0, sign=1.0):
+    send(lse, out_ref, own_ref, kept_ref)
+
+
+def combine(pieces, copies, own=None, keep=True):
     lines = pieces[0].shape[1:]
     olds = () if own is None else (own,)
     kind = jnp.bfloat16 if olds else jnp.float32
     return pl.pallas_call(
-        functools.partial(combine_kernel, (len(pieces), len(olds)), offset, sign),
+        functools.partial(combine_kernel, (len(pieces), len(olds))),
         out_shape=[
             jax.ShapeDtypeStruct((copies, *lines), kind),
-            jax.ShapeDtypeStruct(lines, jnp.float32),
+            *[jax.ShapeDtypeStruct(lines, jnp.float32) for _ in range(keep)],
         ],
         compiler_params=pltpu.CompilerParams(vmem_limit_bytes=VMEM),
         name="combine",
@@ -438,44 +454,55 @@
     chips, cores = lax.axis_size(along), lax.axis_size(core)
     chip, half = lax.axis_index(along), lax.axis_index(core)
     code_copies = chips * cores
-    from_left, from_right = ring_shift(frames, along, 1), ring_shift(frames, along, -1)
+    turn = 1 - 2 * half
+
+    def crossing(step):
+        there = []
+        for k in range(chips):
+            for c in range(cores):
+                there.append((k * cores + c, (k + (1 - 2 * c) * step) % chips * cores + c))
+        return there
+
+    near = lax.ppermute(frames, CODES, crossing(1))
     feature_width = codes.shape[1]
     num_blocks = codes.shape[0] // BLK
     frame_count = pattern.shape[0]
     picked = candidates(pattern, lax.axis_index(CODES) * num_blocks)
     codes = codes.reshape(num_blocks, BLK, feature_width)
-    places = {
-        (k, mine): (((chip - k) % chips) * cores + (half + mine) % cores).reshape(1)
-        for k in (0, 1, chips - 1, 2)
-        for mine in (0, 1)
-    }
-    picks, picked, picked_t, places = lax.optimization_barrier(
-        (picked.reshape(-1), picked, picked.T, places)
-    )
+    places = {}
+    for name, step in (("own", 0), ("near", -turn), ("back", turn), ("far", 2)):
+        places[name, 0] = ((chip + step) % chips * cores + half).reshape(1)
+        places[name, 1] = ((chip - step) % chips * cores + 1 - half).reshape(1)
+    picks, picked, picked_t, places, late = lax.optimization_barrier(
+        (picked.reshape(-1), picked, picked.T, places, frames)
+    )
+    back = lax.ppermute(late, CODES, crossing(-1))
     frames_total = frame_count * BLK * lax.axis_size(FRAMES)
     codes_total = num_blocks * BLK * lax.axis_size(CODES)
     log_ratio = math.log(frames_total / codes_total)
     made = ()
 
-    def use(made, k, mine, *parts):
-        return make_tiles(picks, places[k, mine], parts, codes, code_copies, made)
-
-    other = ring_shift(frames, core, 1)
-    made = use(made, 0, 0, frames)
-    made = use(made, 0, 1, other)
-    from_left, from_right, made = lax.optimization_barrier((from_left, from_right, made))
-    upper, lower = halves(from_left, from_right)
-    upper = ring_shift(upper, along, 1)
-    lower = ring_shift(lower, along, -1)
-    swapped = tuple(ring_shift(block, core, 1) for block in (from_left, from_right))
-    made = use(made, 1, 0, from_left)
-    made = use(made, chips - 1, 0, from_right)
-    made = use(made, 1, 1, swapped[0])
-    made = use(made, chips - 1, 1, swapped[1])
-    upper, lower, made = lax.optimization_barrier((upper, lower, made))
-    swapped = tuple(ring_shift(block, core, 1) for block in (upper, lower))
-    made = use(made, 2, 0, upper, lower)
-    made = use(made, 2, 1, *swapped)
+    def use(made, name, swapped, block):
+        return make_tiles(picks, places[name, swapped], (block,), codes, code_copies, made)
+
+    def swap(block):
+        return ring_shift(block, core, 1)
+
+    made = use(made, "own", 1, swap(frames))
+    made = use(made, "own", 0, frames)
+    near, made = lax.optimization_barrier((near, made))
+    far = lax.ppermute(near, CODES, crossing(1))
+    other = swap(near)
+    made = use(made, "near", 0, near)
+    made = use(made, "near", 1, other)
+    back, made = lax.optimization_barrier((back, made))
+    other = swap(back)
+    made = use(made, "back", 0, back)
+    made = use(made, "back", 1, other)
+    far, made = lax.optimization_barrier((far, made))
+    other = swap(far)
+    made = use(made, "far", 0, far)
+    made = use(made, "far", 1, other)
     exps, logits, high, lse = made
     first, second = FRAMES
 
@@ -487,20 +514,25 @@
     cols = ()
     col_sent = None
     for iteration in range(ITERS):
-        row_potential, pieces, *kept = column_pass(
-            picks, rows, high, picked_t, exps, logits, lax.axis_size(first)
+        last = iteration == ITERS - 1
+        pieces, *kept = column_pass(
+            picks, rows, high, picked_t, exps, logits, lax.axis_size(first), last
         )
         rows = tuple(kept) or rows
         pieces = exchange(pieces, first)
-        pieces, col_sent = combine((pieces,), lax.axis_size(second), col_sent)
+        pieces, *kept = combine((pieces,), lax.axis_size(second), col_sent, keep=not last)
+        col_sent = None if last else kept[0]
         cols = (*cols[:1], exchange(pieces, second))
-        if iteration < ITERS - 1:
-            pieces, row_sent, *kept = row_pass(
-                picks, cols, row_sent, high, picked, exps, logits, code_copies, log_ratio
-            )
+        if not last:
+            keep = iteration < ITERS - 2
+            pieces, *kept = row_pass(
+                picks, cols, row_sent, high, picked, exps, logits, code_copies, log_ratio, keep
+            )
+            if keep:
+                row_sent, *kept = kept
             cols = tuple(kept) or cols
             rows = (rows[0], exchange(pieces, CODES))
-    _, col_potential = combine(cols, 1, None, log_ratio, -1.0)
+    row_potential, col_potential = finish(cols, rows[0], log_ratio)
     return (row_potential.reshape(-1), col_potential.reshape(-1))
 
 

time: 362 us -> 357 us (0.986)
  Pallas kernels: 44.1 us -> 37.2 us
    ppermute x0 -> x3, waiting for transfers between devices: none -> 7.04 us  [the longest x1 3.84 us: shards(): far = lax.ppermute(near, CODES, crossing(1))]
    pallas_call x6, Pallas kernels: 25.9 us -> 20.5 us  [the longest x3 13.9 us: column_pass(): pl.pallas_call(functools.partial(column_kernel, len(pieces), last), grid_...]
    ppermute x9 -> x4, starting transfers between devices: 5.4 us -> 0.19 us  [ring_shift(): lax.ppermute(array, axis, [(k, (k + step) % size) for k in range(size)])]
    ppermute x9 -> x4, waiting for transfers between devices: 4.88 us -> 0.01 us  [ring_shift(): lax.ppermute(array, axis, [(k, (k + step) % size) for k in range(size)])]
    ppermute x0 -> x3, starting transfers between devices: none -> 4.7 us  [the longest x1 1.93 us: shards(): back = lax.ppermute(late, CODES, crossing(-1))]
  transfers between devices with their start and end apart: 9 -> 7, of which waited for: 2 -> 2; matrix products, arithmetic and copies ran while one was open for 0% -> 0% of each run, Pallas kernels for 4% -> 4%
where the time goes in v2:
time: 357 us; the launch traced here: 355 us
  blocking collectives  301 us (84%)
  Pallas kernels  37.2 us (10%)
  waiting for transfers between devices  7.06 us (2%)
  starting transfers between devices  4.89 us (1%)
  local copies, waits for them, and re-layouts  3.61 us (1%)
    all_to_all x9, blocking collectives, exchange(): return lax.all_to_all(pieces, axes, 0, 0, tiled=True)  301 us
    pallas_call x8, Pallas kernels, make_tiles(): pl.pallas_call(functools.partial(tiles_kernel, parts), grid_spec=pltpu.Pr...  16.5 us
    pallas_call x3, Pallas kernels, column_pass(): pl.pallas_call(functools.partial(column_kernel, len(pieces), last), grid_...  13.9 us
  transfers between devices with their start and end apart: 7, of which 2 were waited for; matrix products, arithmetic and copies ran while one was open for 0% of the time, Pallas kernels for 4%

profile of v2, /device:TPU:34, one launch (start us, length us, event | category | flops | bytes accessed | tf_op | source)
XLA Modules:
  0.0 355.3 jit_solution(14589542953557809472)
XLA Ops:
  0.7 1.6 collective-permute-start
  2.3 0.8 convert_reduce_fusion
  3.3 0.1 copy.46
  3.7 2.2 copy-done
  5.9 2.1 make_tiles.8
  7.9 1.0 copy-done.1
  9.0 2.1 make_tiles.9
  11.1 1.9 collective-permute-start.3
  13.1 2.1 make_tiles.10
  15.1 2.1 make_tiles.11
  17.2 3.2 collective-permute-done.3.refs_0_
  20.4 1.2 collective-permute-start.2
  21.6 2.1 make_tiles.12
  23.7 2.1 make_tiles.13
  25.8 3.8 %collective-permute-done.2.refs_0_ = bf16[1024,256]{1,0:T(8,128)(2,1)S(1)} collective-permute-done((bf16[1024,256]{1,0:T(8,128)(2,1)S(1)}, bf16[1024,256]{1,0:T(8,128)(2,1)S(1)}, u32[]{:S(2)}, u32[]{:S(2)}) %collective-permute-start.2) | collective-permute-done | bytes 524320 | tf_op jit(solution)/shard_map/ppermute | solution.py:494
  29.6 2.1 make_tiles.14
  31.7 2.1 make_tiles.15
  33.8 11.7 %all_to_all.45.refs_0_ = f32[8,64,128]{2,1,0:T(8,128)S(1)} all-to-all(f32[8,64,128]{2,1,0:T(8,128)S(1)} %get-tuple-element.131), channel_id=1, replica_groups=mesh['frames_0'=4,'frames_1'=8,'codes_0'=4,'codes_1'=2] {'codes_0','code..., dimensions={0} | all-to-all | bytes 524288 | tf_op jit(solution)/shard_map/all_to_all | solution.py:510
  45.4 4.6 %column_pass.3 = f32[4,64,128]{2,1,0:T(8,128)S(1)} custom-call(s32[512]{0:T(512)S(1)} %and_select_fusion.1.picks, f32[8,64,128]{2,1,0:T(8,128)S(1)} %all_to_all.45.refs_0_, f32[64,128]{1,0:T(8,128)S(1)} %get-tuple-element.132.refs_1_.refs_2_.refs_3_, s32[8,64]{1,0:T(8,128)S(1)} %bitcast_select_fusion.refs_2_.refs_3_, ...), custom_call_target="tpu_custom_call" | custom-call | tf_op jit(solution)/shard_map/column_pass/pallas_call | solution.py:324
  50.1 10.2 %all_to_all.46.refs_0_ = f32[4,64,128]{2,1,0:T(8,128)S(1)} all-to-all(f32[4,64,128]{2,1,0:T(8,128)S(1)} %column_pass.3), channel_id=1, replica_groups=mesh['frames_0'=4,'frames_1'=8,'codes_0'=4,'codes_1'=2] {'frames_0'}, dimensions={0} | all-to-all | bytes 262144 | tf_op jit(solution)/shard_map/all_to_all | solution.py:510
  60.3 17.4 %all_to_all.47.refs_0_ = f32[8,64,128]{2,1,0:T(8,128)S(1)} all-to-all(f32[8,64,128]{2,1,0:T(8,128)S(1)} %get-tuple-element.136), channel_id=1, replica_groups=mesh['frames_0'=4,'frames_1'=8,'codes_0'=4,'codes_1'=2] {'frames_1'}, dimensions={0} | all-to-all | bytes 524288 | tf_op jit(solution)/shard_map/all_to_all | solution.py:510
  77.7 3.0 row_pass.2
  80.7 86.2 %all_to_all.48.refs_1_ = bf16[8,64,128]{2,1,0:T(8,128)(2,1)S(1)} all-to-all(bf16[8,64,128]{2,1,0:T(8,128)(2,1)S(1)} %get-tuple-element.139), channel_id=1, replica_groups=mesh['frames_0'=4,'frames_1'=8,'codes_0'=4,'codes_1'=2] {'codes_0','code..., dimensions={0} | all-to-all | bytes 262144 | tf_op jit(solution)/shard_map/all_to_all | solution.py:510
  166.9 4.6 %column_pass.4 = (f32[4,64,128]{2,1,0:T(8,128)S(1)}, f32[8,64,128]{2,1,0:T(8,128)S(1)}) custom-call(s32[512]{0:T(512)S(1)} %and_select_fusion.1.picks, f32[8,64,128]{2,1,0:T(8,128)S(1)} %all_to_all.45.refs_0_, bf16[8,64,128]{2,1,0:T(8,128)(2,1)S(1)} %all_to_all.48.refs_1_, f32[64,128]{1,0:T(8,128)S(1)} %get-tuple-element.132.refs_1_.refs_2_.refs_3_, ...), custom_call_target="tpu_custom_call" | custom-call | tf_op jit(solution)/shard_map/column_pass/pallas_call | solution.py:324
  171.6 9.7 %all_to_all.49.refs_0_ = f32[4,64,128]{2,1,0:T(8,128)S(1)} all-to-all(f32[4,64,128]{2,1,0:T(8,128)S(1)} %get-tuple-element.140), channel_id=1, replica_groups=mesh['frames_0'=4,'frames_1'=8,'codes_0'=4,'codes_1'=2] {'frames_0'}, dimensions={0} | all-to-all | bytes 262144 | tf_op jit(solution)/shard_map/all_to_all | solution.py:510
  181.3 12.5 %all_to_all.50.refs_1_ = bf16[8,64,128]{2,1,0:T(8,128)(2,1)S(1)} all-to-all(bf16[8,64,128]{2,1,0:T(8,128)(2,1)S(1)} %get-tuple-element.142), channel_id=1, replica_groups=mesh['frames_0'=4,'frames_1'=8,'codes_0'=4,'codes_1'=2] {'frames_1'}, dimensions={0} | all-to-all | bytes 262144 | tf_op jit(solution)/shard_map/all_to_all | solution.py:510
  193.8 3.0 row_pass.3
  196.8 89.0 %all_to_all.51.refs_1_ = bf16[8,64,128]{2,1,0:T(8,128)(2,1)S(1)} all-to-all(bf16[8,64,128]{2,1,0:T(8,128)(2,1)S(1)} %get-tuple-element.146), channel_id=1, replica_groups=mesh['frames_0'=4,'frames_1'=8,'codes_0'=4,'codes_1'=2] {'codes_0','code..., dimensions={0} | all-to-all | bytes 262144 | tf_op jit(solution)/shard_map/all_to_all | solution.py:510
  285.7 4.6 %column_pass.5 = (f32[4,64,128]{2,1,0:T(8,128)S(1)}, f32[64,128]{1,0:T(8,128)S(1)}) custom-call(s32[512]{0:T(512)S(1)} %and_select_fusion.1.picks, f32[8,64,128]{2,1,0:T(8,128)S(1)} %get-tuple-element.145.refs_0_, bf16[8,64,128]{2,1,0:T(8,128)(2,1)S(1)} %all_to_all.51.refs_1_, f32[64,128]{1,0:T(8,128)S(1)} %get-tuple-element.132.refs_1_.refs_2_.refs_3_, ...), custom_call_target="tpu_custom_call" | custom-call | tf_op jit(solution)/shard_map/column_pass/pallas_call | solution.py:324
  290.4 46.7 %all_to_all.52.refs_0_ = f32[4,64,128]{2,1,0:T(8,128)S(1)} all-to-all(f32[4,64,128]{2,1,0:T(8,128)S(1)} %get-tuple-element.147), channel_id=1, replica_groups=mesh['frames_0'=4,'frames_1'=8,'codes_0'=4,'codes_1'=2] {'frames_0'}, dimensions={0} | all-to-all | bytes 262144 | tf_op jit(solution)/shard_map/all_to_all | solution.py:510
  337.1 17.4 %all_to_all.53.change_ref = bf16[8,64,128]{2,1,0:T(8,128)(2,1)S(1)} all-to-all(bf16[8,64,128]{2,1,0:T(8,128)(2,1)S(1)} %combine.7), channel_id=1, replica_groups=mesh['frames_0'=4,'frames_1'=8,'codes_0'=4,'codes_1'=2] {'frames_1'}, dimensions={0} | all-to-all | bytes 262144 | tf_op jit(solution)/shard_map/all_to_all | solution.py:510
  354.6 0.7 finish.1
  (26 shorter events, 0.8 us)
Async XLA Ops:
  0.6 3.0 collective-permute-start.1
  0.7 10.3 %collective-permute-start = (bf16[1024,256]{1,0:T(8,128)(2,1)}, bf16[1024,256]{1,0:T(8,128)(2,1)S(1)}, u32[]{:S(2)}, u32[]{:S(2)}) collective-permute-start(bf16[1024,256]{1,0:T(8,128)(2,1)} %refs_0_.1), channel_id=1, source_target_pairs={{0,2},{1,7},{2,4},{3,1},{4,6},{5,3},{6,0},{7,5},{8,10},{9,15},{10,... | collective-permute-start | bytes 1572872 | tf_op jit(solution)/shard_map/ppermute | solution.py:466
  3.7 2.2 copy-start
  7.9 1.1 copy-start.1
  11.0 4.1 %collective-permute-start.4 = (bf16[1024,256]{1,0:T(8,128)(2,1)S(1)}, bf16[1024,256]{1,0:T(8,128)(2,1)S(1)}, u32[]{:S(2)}, u32[]{:S(2)}) collective-permute-start(bf16[1024,256]{1,0:T(8,128)(2,1)S(1)} %collective-permute-done.refs_0_), channel_id=1, source_target_pairs={{0,1},{1,0},{2,3},{3,2},{4,5},{5,4},{6,7},{7,6},{8,9},{9,8},{10,11... | collective-permute-start | bytes 1572872 | tf_op jit(solution)/shard_map/ppermute | solution.py:407
  11.1 9.3 %collective-permute-start.3 = (bf16[1024,256]{1,0:T(8,128)(2,1)S(1)}, bf16[1024,256]{1,0:T(8,128)(2,1)S(1)}, u32[]{:S(2)}, u32[]{:S(2)}) collective-permute-start(bf16[1024,256]{1,0:T(8,128)(2,1)S(1)} %copy-done.1), channel_id=1, source_target_pairs={{0,6},{1,3},{2,0},{3,5},{4,2},{5,7},{6,4},{7,1},{8,14},{9,11},{10,... | collective-permute-start | bytes 1572872 | tf_op jit(solution)/shard_map/ppermute | solution.py:479
  20.4 3.3 collective-permute-start.5
  20.4 9.2 %collective-permute-start.2 = (bf16[1024,256]{1,0:T(8,128)(2,1)S(1)}, bf16[1024,256]{1,0:T(8,128)(2,1)S(1)}, u32[]{:S(2)}, u32[]{:S(2)}) collective-permute-start(bf16[1024,256]{1,0:T(8,128)(2,1)S(1)} %collective-permute-done.refs_0_), channel_id=1, source_target_pairs={{0,2},{1,7},{2,4},{3,1},{4,6},{5,3},{6,0},{7,5},{8,10},{9,15},{10,... | collective-permute-start | bytes 1572872 | tf_op jit(solution)/shard_map/ppermute | solution.py:494
  29.6 2.1 collective-permute-start.6

commit v3 on v2

--- a/solution.py
+++ b/solution.py
@@ -32,10 +32,10 @@
         held = PER // parts
         at = (b % held) * BLK
         block = refs[b // held][at : at + BLK, :] * jnp.bfloat16(2.0)
-        first = picks[(chunk[0] * PER + b) * 8]
+        first = picks[0, chunk[0] * PER + b]
         chosen, filled = [], []
         for s in range(CAP):
-            pick = picks[(chunk[0] * PER + b) * 8 + s]
+            pick = picks[s, chunk[0] * PER + b]
             chosen.append(codes_ref[jnp.maximum(jnp.where(pick >= 0, pick, first), 0)])
             filled.append(jnp.where(pick >= 0, 1.0, 0.0))
         top = None
@@ -153,7 +153,7 @@
             b = index // CAP
             s = index - b * CAP
             row = g * PER + b
-            pick = picks[row * 8 + s]
+            pick = picks[s, row]
 
             @pl.when(pick >= 0)
             def _():
@@ -391,15 +391,38 @@
     )(picks, *pieces, own, high, picks_v, exps, logits)
 
 
-def candidates(pattern, low_block):
-    _, slots = pattern.shape
-    first = jnp.sum((pattern < low_block).astype(jnp.int32), axis=1)
-    position = first[:, None] + jnp.arange(8, dtype=jnp.int32)[None, :]
-    here = position[:, :, None] == jnp.arange(slots, dtype=jnp.int32)[None, None, :]
-    offset = pattern - low_block
-    found = jnp.max(jnp.where(here, offset[:, None, :], -1), axis=2)
-    fits = (found < GB) & (jnp.arange(8, dtype=jnp.int32)[None, :] < CAP)
-    return jnp.where(fits, found, -1)
+def tables_kernel(low_ref, pattern_ref, picked_ref, table_ref):
+    low = low_ref[0]
+    pattern = pattern_ref[...]
+    rows, slots = pattern.shape
+    first = jnp.sum(jnp.where(pattern < low, 1.0, 0.0), axis=1, keepdims=True)
+    position = lax.broadcasted_iota(jnp.int32, (rows, slots), 1).astype(jnp.float32) - first
+    offset = (pattern - low).astype(jnp.float32)
+    lane = lax.broadcasted_iota(jnp.int32, (rows, BLK), 1)
+    picked = jnp.full((rows, BLK), -1.0, jnp.float32)
+    for s in range(CAP):
+        found = jnp.max(jnp.where(position == s, offset, -1.0), axis=1, keepdims=True)
+        found = jnp.where(found < GB, found, -1.0)
+        picked = jnp.where(lane == s, found, picked)
+    picked_ref[...] = picked[:, :8].astype(jnp.int32)
+    table_ref[...] = jnp.transpose(picked)[:8, :].astype(jnp.int32)
+
+
+def tables(low, pattern):
+    rows = pattern.shape[0]
+    near = pl.BlockSpec(memory_space=pltpu.VMEM)
+    return pl.pallas_call(
+        tables_kernel,
+        in_specs=[pl.BlockSpec(memory_space=pltpu.SMEM), near],
+        out_specs=[near, near],
+        out_shape=[
+            jax.ShapeDtypeStruct((rows, 8), jnp.int32),
+            jax.ShapeDtypeStruct((8, rows), jnp.int32),
+        ],
+        cost_estimate=pl.CostEstimate(flops=0, bytes_accessed=1 << 23, transcendentals=0),
+        compiler_params=pltpu.CompilerParams(vmem_limit_bytes=VMEM),
+        name="tables",
+    )(low, pattern)
 
 
 def ring_shift(array, axis, step):
@@ -467,16 +490,15 @@
     feature_width = codes.shape[1]
     num_blocks = codes.shape[0] // BLK
     frame_count = pattern.shape[0]
-    picked = candidates(pattern, lax.axis_index(CODES) * num_blocks)
-    codes = codes.reshape(num_blocks, BLK, feature_width)
     places = {}
     for name, step in (("own", 0), ("near", -turn), ("back", turn), ("far", 2)):
         places[name, 0] = ((chip + step) % chips * cores + half).reshape(1)
         places[name, 1] = ((chip - step) % chips * cores + 1 - half).reshape(1)
-    picks, picked, picked_t, places, late = lax.optimization_barrier(
-        (picked.reshape(-1), picked, picked.T, places, frames)
-    )
-    back = lax.ppermute(late, CODES, crossing(-1))
+    low = (lax.axis_index(CODES) * num_blocks).reshape(1)
+    places, low = lax.optimization_barrier((places, low))
+    picked, picks = tables(low, pattern)
+    picked_t = picks
+    codes = codes.reshape(num_blocks, BLK, feature_width)
     frames_total = frame_count * BLK * lax.axis_size(FRAMES)
     codes_total = num_blocks * BLK * lax.axis_size(CODES)
     log_ratio = math.log(frames_total / codes_total)
@@ -489,6 +511,8 @@
         return ring_shift(block, core, 1)
 
     made = use(made, "own", 1, swap(frames))
+    late, made = lax.optimization_barrier((frames, made))
+    back = lax.ppermute(late, CODES, crossing(-1))
     made = use(made, "own", 0, frames)
     near, made = lax.optimization_barrier((near, made))
     far = lax.ppermute(near, CODES, crossing(1))

time: 357 us -> 360 us (level)
  no operation moved by 1% of the time
where the time goes in v3:
time: 360 us; the launch traced here: 358 us
  blocking collectives  303 us (84%)
  Pallas kernels  37.9 us (11%)
  waiting for transfers between devices  6.92 us (2%)
  starting transfers between devices  4.88 us (1%)
  local copies, waits for them, and re-layouts  4.05 us (1%)
    all_to_all x9, blocking collectives, exchange(): return lax.all_to_all(pieces, axes, 0, 0, tiled=True)  303 us
    pallas_call x8, Pallas kernels, make_tiles(): pl.pallas_call(functools.partial(tiles_kernel, parts), grid_spec=pltpu.Pr...  16.8 us
    pallas_call x3, Pallas kernels, column_pass(): pl.pallas_call(functools.partial(column_kernel, len(pieces), last), grid_...  14 us
  transfers between devices with their start and end apart: 7, of which 2 were waited for; matrix products, arithmetic and copies ran while one was open for 0% of the time, Pallas kernels for 4%

profile of v3, /device:TPU:34, one launch (start us, length us, event | category | flops | bytes accessed | tf_op | source)
XLA Modules:
  0.0 357.5 jit_solution(6008739099251802263)
XLA Ops:
  0.7 1.6 collective-permute-start
  2.3 0.8 copy.33.pattern_ref
  3.1 0.3 tables.1
  3.4 2.2 copy-done
  5.6 2.1 make_tiles.8
  7.7 1.0 copy-done.1
  8.7 2.1 make_tiles.9
  10.9 1.9 collective-permute-start.3
  12.9 2.1 make_tiles.10
  15.0 2.1 make_tiles.11
  17.1 3.1 collective-permute-done.3.refs_0_
  20.2 1.2 collective-permute-start.2
  21.4 2.1 make_tiles.12
  23.5 2.1 make_tiles.13
  25.6 3.8 %collective-permute-done.2.refs_0_ = bf16[1024,256]{1,0:T(8,128)(2,1)S(1)} collective-permute-done((bf16[1024,256]{1,0:T(8,128)(2,1)S(1)}, bf16[1024,256]{1,0:T(8,128)(2,1)S(1)}, u32[]{:S(2)}, u32[]{:S(2)}) %collective-permute-start.2) | collective-permute-done | bytes 524320 | tf_op jit(solution)/shard_map/ppermute | solution.py:518
  29.4 2.1 make_tiles.14
  31.5 2.1 make_tiles.15
  33.6 11.8 %all_to_all.45.refs_0_ = f32[8,64,128]{2,1,0:T(8,128)S(1)} all-to-all(f32[8,64,128]{2,1,0:T(8,128)S(1)} %get-tuple-element.140), channel_id=1, replica_groups=mesh['frames_0'=4,'frames_1'=8,'codes_0'=4,'codes_1'=2] {'codes_0','code..., dimensions={0} | all-to-all | bytes 524288 | tf_op jit(solution)/shard_map/all_to_all | solution.py:534
  45.5 4.6 %column_pass.3 = f32[4,64,128]{2,1,0:T(8,128)S(1)} custom-call(s32[8,64]{1,0:T(8,128)S(1)} %get-tuple-element.82.picks.refs_2_.refs_3_, f32[8,64,128]{2,1,0:T(8,128)S(1)} %all_to_all.45.refs_0_, f32[64,128]{1,0:T(8,128)S(1)} %get-tuple-element.141.refs_1_.refs_2_.refs_3_, s32[8,64]{1,0:T(8,128)S(1)} %get-tuple-element.82.picks.refs_2_.refs_3_, ...), custom_call_target="tpu_custom_call" | custom-call | tf_op jit(solution)/shard_map/column_pass/pallas_call | solution.py:324
  50.1 10.2 %all_to_all.46.refs_0_ = f32[4,64,128]{2,1,0:T(8,128)S(1)} all-to-all(f32[4,64,128]{2,1,0:T(8,128)S(1)} %column_pass.3), channel_id=1, replica_groups=mesh['frames_0'=4,'frames_1'=8,'codes_0'=4,'codes_1'=2] {'frames_0'}, dimensions={0} | all-to-all | bytes 262144 | tf_op jit(solution)/shard_map/all_to_all | solution.py:534
  60.4 17.4 %all_to_all.47.refs_0_ = f32[8,64,128]{2,1,0:T(8,128)S(1)} all-to-all(f32[8,64,128]{2,1,0:T(8,128)S(1)} %get-tuple-element.144), channel_id=1, replica_groups=mesh['frames_0'=4,'frames_1'=8,'codes_0'=4,'codes_1'=2] {'frames_1'}, dimensions={0} | all-to-all | bytes 524288 | tf_op jit(solution)/shard_map/all_to_all | solution.py:534
  77.8 3.0 row_pass.2
  80.8 87.0 %all_to_all.48.refs_1_ = bf16[8,64,128]{2,1,0:T(8,128)(2,1)S(1)} all-to-all(bf16[8,64,128]{2,1,0:T(8,128)(2,1)S(1)} %get-tuple-element.147), channel_id=1, replica_groups=mesh['frames_0'=4,'frames_1'=8,'codes_0'=4,'codes_1'=2] {'codes_0','code..., dimensions={0} | all-to-all | bytes 262144 | tf_op jit(solution)/shard_map/all_to_all | solution.py:534
  167.9 4.7 %column_pass.4 = (f32[4,64,128]{2,1,0:T(8,128)S(1)}, f32[8,64,128]{2,1,0:T(8,128)S(1)}) custom-call(s32[8,64]{1,0:T(8,128)S(1)} %get-tuple-element.82.picks.refs_2_.refs_3_, f32[8,64,128]{2,1,0:T(8,128)S(1)} %all_to_all.45.refs_0_, bf16[8,64,128]{2,1,0:T(8,128)(2,1)S(1)} %all_to_all.48.refs_1_, f32[64,128]{1,0:T(8,128)S(1)} %get-tuple-element.141.refs_1_.refs_2_.refs_3_, ...), custom_call_target="tpu_custom_call" | custom-call | tf_op jit(solution)/shard_map/column_pass/pallas_call | solution.py:324
  172.5 9.7 %all_to_all.49.refs_0_ = f32[4,64,128]{2,1,0:T(8,128)S(1)} all-to-all(f32[4,64,128]{2,1,0:T(8,128)S(1)} %get-tuple-element.148), channel_id=1, replica_groups=mesh['frames_0'=4,'frames_1'=8,'codes_0'=4,'codes_1'=2] {'frames_0'}, dimensions={0} | all-to-all | bytes 262144 | tf_op jit(solution)/shard_map/all_to_all | solution.py:534
  182.3 12.5 %all_to_all.50.refs_1_ = bf16[8,64,128]{2,1,0:T(8,128)(2,1)S(1)} all-to-all(bf16[8,64,128]{2,1,0:T(8,128)(2,1)S(1)} %get-tuple-element.150), channel_id=1, replica_groups=mesh['frames_0'=4,'frames_1'=8,'codes_0'=4,'codes_1'=2] {'frames_1'}, dimensions={0} | all-to-all | bytes 262144 | tf_op jit(solution)/shard_map/all_to_all | solution.py:534
  194.8 3.0 row_pass.3
  197.8 89.8 %all_to_all.51.refs_1_ = bf16[8,64,128]{2,1,0:T(8,128)(2,1)S(1)} all-to-all(bf16[8,64,128]{2,1,0:T(8,128)(2,1)S(1)} %get-tuple-element.154), channel_id=1, replica_groups=mesh['frames_0'=4,'frames_1'=8,'codes_0'=4,'codes_1'=2] {'codes_0','code..., dimensions={0} | all-to-all | bytes 262144 | tf_op jit(solution)/shard_map/all_to_all | solution.py:534
  287.6 4.7 %column_pass.5 = (f32[4,64,128]{2,1,0:T(8,128)S(1)}, f32[64,128]{1,0:T(8,128)S(1)}) custom-call(s32[8,64]{1,0:T(8,128)S(1)} %get-tuple-element.82.picks.refs_2_.refs_3_, f32[8,64,128]{2,1,0:T(8,128)S(1)} %get-tuple-element.153.refs_0_, bf16[8,64,128]{2,1,0:T(8,128)(2,1)S(1)} %all_to_all.51.refs_1_, f32[64,128]{1,0:T(8,128)S(1)} %get-tuple-element.141.refs_1_.refs_2_.refs_3_, ...), custom_call_target="tpu_custom_call" | custom-call | tf_op jit(solution)/shard_map/column_pass/pallas_call | solution.py:324
  292.2 47.1 %all_to_all.52.refs_0_ = f32[4,64,128]{2,1,0:T(8,128)S(1)} all-to-all(f32[4,64,128]{2,1,0:T(8,128)S(1)} %get-tuple-element.155), channel_id=1, replica_groups=mesh['frames_0'=4,'frames_1'=8,'codes_0'=4,'codes_1'=2] {'frames_0'}, dimensions={0} | all-to-all | bytes 262144 | tf_op jit(solution)/shard_map/all_to_all | solution.py:534
  339.4 17.4 %all_to_all.53.change_ref = bf16[8,64,128]{2,1,0:T(8,128)(2,1)S(1)} all-to-all(bf16[8,64,128]{2,1,0:T(8,128)(2,1)S(1)} %combine.7), channel_id=1, replica_groups=mesh['frames_0'=4,'frames_1'=8,'codes_0'=4,'codes_1'=2] {'frames_1'}, dimensions={0} | all-to-all | bytes 262144 | tf_op jit(solution)/shard_map/all_to_all | solution.py:534
  356.8 0.7 finish.1
  (15 shorter events, 0.4 us)
Async XLA Ops:
  0.6 2.8 collective-permute-start.1
  0.7 10.1 %collective-permute-start = (bf16[1024,256]{1,0:T(8,128)(2,1)}, bf16[1024,256]{1,0:T(8,128)(2,1)S(1)}, u32[]{:S(2)}, u32[]{:S(2)}) collective-permute-start(bf16[1024,256]{1,0:T(8,128)(2,1)} %refs_0_.1), channel_id=1, source_target_pairs={{0,2},{1,7},{2,4},{3,1},{4,6},{5,3},{6,0},{7,5},{8,10},{9,15},{10,... | collective-permute-start | bytes 1572872 | tf_op jit(solution)/shard_map/ppermute | solution.py:489
  3.4 2.2 copy-start
  7.7 1.1 copy-start.1
  10.8 4.1 %collective-permute-start.4 = (bf16[1024,256]{1,0:T(8,128)(2,1)S(1)}, bf16[1024,256]{1,0:T(8,128)(2,1)S(1)}, u32[]{:S(2)}, u32[]{:S(2)}) collective-permute-start(bf16[1024,256]{1,0:T(8,128)(2,1)S(1)} %collective-permute-done.refs_0_), channel_id=1, source_target_pairs={{0,1},{1,0},{2,3},{3,2},{4,5},{5,4},{6,7},{7,6},{8,9},{9,8},{10,11... | collective-permute-start | bytes 1572872 | tf_op jit(solution)/shard_map/ppermute | solution.py:430
  10.9 9.3 %collective-permute-start.3 = (bf16[1024,256]{1,0:T(8,128)(2,1)S(1)}, bf16[1024,256]{1,0:T(8,128)(2,1)S(1)}, u32[]{:S(2)}, u32[]{:S(2)}) collective-permute-start(bf16[1024,256]{1,0:T(8,128)(2,1)S(1)} %copy-done.1), channel_id=1, source_target_pairs={{0,6},{1,3},{2,0},{3,5},{4,2},{5,7},{6,4},{7,1},{8,14},{9,11},{10,... | collective-permute-start | bytes 1572872 | tf_op jit(solution)/shard_map/ppermute | solution.py:515
  20.2 3.3 collective-permute-start.5
  20.2 9.2 %collective-permute-start.2 = (bf16[1024,256]{1,0:T(8,128)(2,1)S(1)}, bf16[1024,256]{1,0:T(8,128)(2,1)S(1)}, u32[]{:S(2)}, u32[]{:S(2)}) collective-permute-start(bf16[1024,256]{1,0:T(8,128)(2,1)S(1)} %collective-permute-done.refs_0_), channel_id=1, source_target_pairs={{0,2},{1,7},{2,4},{3,1},{4,6},{5,3},{6,0},{7,5},{8,10},{9,15},{10,... | collective-permute-start | bytes 1572872 | tf_op jit(solution)/shard_map/ppermute | solution.py:518
  29.4 2.1 collective-permute-start.6

commit v4 on v3

--- a/solution.py
+++ b/solution.py
@@ -15,7 +15,7 @@
 CAP = 6
 ITERS = 3
 PER = 8
-STEP = 4
+STEP = 8
 CODES = ("codes_0", "codes_1")
 FRAMES = ("frames_0", "frames_1")
 FRAMES_CODES = ("frames_0", "frames_1", "codes_0", "codes_1")
@@ -23,7 +23,7 @@
 NEG_FILL = -1e30
 NEG_ROW = -1e29
 SMALL = 1e-26
-VMEM = 14 * 1024 * 1024
+VMEM = 18 * 1024 * 1024
 
 
 def tiles_kernel(parts, picks, chunk, codes_ref, *refs):
@@ -110,26 +110,22 @@
     return high + jnp.log(total)
 
 
-def arrived(refs, kept_ref=None):
-    if len(refs) == 1:
-        return [refs[0][k] for k in range(refs[0].shape[0])]
+def arrived(refs, kept_ref=None, base=0.0):
     pieces = []
     for k in range(refs[0].shape[0]):
-        pieces.append(refs[0][k] + refs[1][k].astype(jnp.float32))
+        piece = refs[-1][k].astype(jnp.float32)
+        piece = piece + (refs[0][k] if len(refs) == 2 else base)
+        pieces.append(piece)
         if kept_ref is not None:
-            kept_ref[k] = pieces[k]
+            kept_ref[k] = piece
     return pieces
 
 
-def send(piece, out_ref, own_ref=None, kept_ref=None):
-    if own_ref is None:
-        change = piece
-        if kept_ref is not None:
-            kept_ref[...] = piece
-    else:
-        change = (piece - own_ref[...]).astype(jnp.bfloat16)
-        if kept_ref is not None:
-            kept_ref[...] = own_ref[...] + change.astype(jnp.float32)
+def send(piece, out_ref, own_ref=None, kept_ref=None, base=0.0):
+    before = base if own_ref is None else own_ref[...]
+    change = (piece - before).astype(out_ref.dtype)
+    if kept_ref is not None:
+        kept_ref[...] = before + change.astype(jnp.float32)
     for k in range(out_ref.shape[0]):
         out_ref[k] = change
 
@@ -246,18 +242,18 @@
         send(lse_ref[...], out_ref)
 
 
-def row_kernel(pieces, keep, log_ratio, picks, *refs):
+def row_kernel(pieces, keep, log_ratio, base, picks, *refs):
     piece_refs, (own_ref, high_ref, picks_ref, exp_ref, logit_ref, out_ref), refs = (
         refs[:pieces], refs[pieces : pieces + 6], refs[pieces + 6 :]
     )
     sent_ref = refs[0] if keep else None
-    kept_ref = refs[keep] if pieces == 2 else None
+    kept_ref = refs[keep]
     col_ref, scale_ref, sums_ref, peak_ref, lse_ref, block_ref, top_ref, total_ref = refs[-8:]
     group = pl.program_id(0)
 
     @pl.when(group == 0)
     def _():
-        col = log_ratio - log_sum(arrived(piece_refs, kept_ref))
+        col = log_ratio - log_sum(arrived(piece_refs, kept_ref, base))
         col_ref[...] = col
         peak = jnp.max(col)
         peak_ref[0] = peak
@@ -351,17 +347,16 @@
     )(picks, *pieces, high, picks_t, exps, logits)
 
 
-def row_pass(picks, pieces, own, high, picks_v, exps, logits, copies, log_ratio, keep):
+def row_pass(picks, pieces, own, high, picks_v, exps, logits, copies, log_ratio, base, keep):
     groups = exps.shape[0] // PER
     rows = high.shape[0]
-    kept = pieces[:1] if len(pieces) == 2 else ()
     outs = [
         jax.ShapeDtypeStruct((copies, rows, BLK), jnp.bfloat16),
         *[jax.ShapeDtypeStruct((rows, BLK), jnp.float32) for _ in range(keep)],
-        *[jax.ShapeDtypeStruct(piece.shape, piece.dtype) for piece in kept],
+        jax.ShapeDtypeStruct(pieces[0].shape, jnp.float32),
     ]
     return pl.pallas_call(
-        functools.partial(row_kernel, len(pieces), keep, log_ratio),
+        functools.partial(row_kernel, len(pieces), keep, log_ratio, base),
         grid_spec=pltpu.PrefetchScalarGridSpec(
             num_scalar_prefetch=1,
             grid=(groups // STEP,),
@@ -447,29 +442,24 @@
     )(*cols, row)
 
 
-def combine_kernel(counts, *refs):
-    pieces, olds = counts
-    lse = log_sum(arrived(refs[:pieces]))
-    old_refs, out_ref, kept_refs = (
-        refs[pieces : pieces + olds], refs[pieces + olds], refs[pieces + olds + 1 :]
-    )
-    own_ref, kept_ref = (*old_refs, None)[0], (*kept_refs, None)[0]
-    send(lse, out_ref, own_ref, kept_ref)
-
-
-def combine(pieces, copies, own=None, keep=True):
-    lines = pieces[0].shape[1:]
+def combine_kernel(olds, base, pieces_ref, *refs):
+    own_ref = refs[0] if olds else None
+    kept_ref = (*refs[olds + 1 :], None)[0]
+    send(log_sum(arrived((pieces_ref,))), refs[olds], own_ref, kept_ref, base)
+
+
+def combine(pieces, copies, own=None, keep=True, base=0.0, kind=jnp.bfloat16):
+    lines = pieces.shape[1:]
     olds = () if own is None else (own,)
-    kind = jnp.bfloat16 if olds else jnp.float32
     return pl.pallas_call(
-        functools.partial(combine_kernel, (len(pieces), len(olds))),
+        functools.partial(combine_kernel, len(olds), base),
         out_shape=[
             jax.ShapeDtypeStruct((copies, *lines), kind),
             *[jax.ShapeDtypeStruct(lines, jnp.float32) for _ in range(keep)],
         ],
         compiler_params=pltpu.CompilerParams(vmem_limit_bytes=VMEM),
         name="combine",
-    )(*pieces, *olds)
+    )(pieces, *olds)
 
 
 def shards(frames, codes, pattern):
@@ -533,7 +523,8 @@
     def exchange(pieces, axes):
         return lax.all_to_all(pieces, axes, 0, 0, tiled=True)
 
-    pieces, row_sent = combine((lse[None],), code_copies)
+    base = log_ratio - math.log(lax.axis_size(second))
+    pieces, row_sent = combine(lse[None], code_copies, kind=jnp.float32)
     rows = (exchange(pieces, CODES),)
     cols = ()
     col_sent = None
@@ -544,17 +535,17 @@
         )
         rows = tuple(kept) or rows
         pieces = exchange(pieces, first)
-        pieces, *kept = combine((pieces,), lax.axis_size(second), col_sent, keep=not last)
+        pieces, *kept = combine(pieces, lax.axis_size(second), col_sent, not last, base)
         col_sent = None if last else kept[0]
-        cols = (*cols[:1], exchange(pieces, second))
+        cols = (*cols, exchange(pieces, second))
         if not last:
             keep = iteration < ITERS - 2
             pieces, *kept = row_pass(
-                picks, cols, row_sent, high, picked, exps, logits, code_copies, log_ratio, keep
+                picks, cols, row_sent, high, picked, exps, logits, code_copies, log_ratio, base, keep
             )
             if keep:
                 row_sent, *kept = kept
-            cols = tuple(kept) or cols
+            cols = tuple(kept)
             rows = (rows[0], exchange(pieces, CODES))
     row_potential, col_potential = finish(cols, rows[0], log_ratio)
     return (row_potential.reshape(-1), col_potential.reshape(-1))

time: 360 us -> 357 us (level)
  no operation moved by 1% of the time
where the time goes in v4:
time: 357 us; the launch traced here: 355 us
  blocking collectives  301 us (84%)
  Pallas kernels  36.9 us (10%)
  waiting for transfers between devices  6.92 us (2%)
  starting transfers between devices  4.88 us (1%)
  local copies, waits for them, and re-layouts  4.05 us (1%)
    all_to_all x9, blocking collectives, exchange(): return lax.all_to_all(pieces, axes, 0, 0, tiled=True)  301 us
    pallas_call x8, Pallas kernels, make_tiles(): pl.pallas_call(functools.partial(tiles_kernel, parts), grid_spec=pltpu.Pr...  16.8 us
    pallas_call x3, Pallas kernels, column_pass(): pl.pallas_call(functools.partial(column_kernel, len(pieces), last), grid_...  13.4 us
  transfers between devices with their start and end apart: 7, of which 2 were waited for; matrix products, arithmetic and copies ran while one was open for 0% of the time, Pallas kernels for 4%

profile of v4, /device:TPU:34, one launch (start us, length us, event | category | flops | bytes accessed | tf_op | source)
XLA Modules:
  0.0 355.0 jit_solution(1723099162801358029)
XLA Ops:
  0.7 1.6 collective-permute-start
  2.3 0.8 copy.33.pattern_ref
  3.1 0.3 tables.1
  3.4 2.2 copy-done
  5.6 2.1 make_tiles.8
  7.7 1.0 copy-done.1
  8.7 2.1 make_tiles.9
  10.9 1.9 collective-permute-start.3
  12.9 2.1 make_tiles.10
  15.0 2.1 make_tiles.11
  17.1 3.1 collective-permute-done.3.refs_0_
  20.2 1.2 collective-permute-start.2
  21.4 2.1 make_tiles.12
  23.5 2.1 make_tiles.13
  25.6 3.8 %collective-permute-done.2.refs_0_ = bf16[1024,256]{1,0:T(8,128)(2,1)S(1)} collective-permute-done((bf16[1024,256]{1,0:T(8,128)(2,1)S(1)}, bf16[1024,256]{1,0:T(8,128)(2,1)S(1)}, u32[]{:S(2)}, u32[]{:S(2)}) %collective-permute-start.2) | collective-permute-done | bytes 524320 | tf_op jit(solution)/shard_map/ppermute | solution.py:508
  29.4 2.1 make_tiles.14
  31.5 2.1 make_tiles.15
  33.6 11.8 %all_to_all.45.refs_0_ = f32[8,64,128]{2,1,0:T(8,128)S(1)} all-to-all(f32[8,64,128]{2,1,0:T(8,128)S(1)} %get-tuple-element.141), channel_id=1, replica_groups=mesh['frames_0'=4,'frames_1'=8,'codes_0'=4,'codes_1'=2] {'codes_0','code..., dimensions={0} | all-to-all | bytes 524288 | tf_op jit(solution)/shard_map/all_to_all | solution.py:524
  45.5 4.4 %column_pass.3 = f32[4,64,128]{2,1,0:T(8,128)S(1)} custom-call(s32[8,64]{1,0:T(8,128)S(1)} %get-tuple-element.83.picks.refs_2_.refs_3_, f32[8,64,128]{2,1,0:T(8,128)S(1)} %all_to_all.45.refs_0_, f32[64,128]{1,0:T(8,128)S(1)} %get-tuple-element.142.refs_1_.refs_2_.refs_3_, s32[8,64]{1,0:T(8,128)S(1)} %get-tuple-element.83.picks.refs_2_.refs_3_, ...), custom_call_target="tpu_custom_call" | custom-call | tf_op jit(solution)/shard_map/column_pass/pallas_call | solution.py:320
  49.9 10.2 %all_to_all.46.pieces_ref = f32[4,64,128]{2,1,0:T(8,128)S(1)} all-to-all(f32[4,64,128]{2,1,0:T(8,128)S(1)} %column_pass.3), channel_id=1, replica_groups=mesh['frames_0'=4,'frames_1'=8,'codes_0'=4,'codes_1'=2] {'frames_0'}, dimensions={0} | all-to-all | bytes 262144 | tf_op jit(solution)/shard_map/all_to_all | solution.py:524
  60.2 16.0 %all_to_all.47.refs_0_ = bf16[8,64,128]{2,1,0:T(8,128)(2,1)S(1)} all-to-all(bf16[8,64,128]{2,1,0:T(8,128)(2,1)S(1)} %get-tuple-element.145), channel_id=1, replica_groups=mesh['frames_0'=4,'frames_1'=8,'codes_0'=4,'codes_1'=2] {'frames_1'}, dimensions={0} | all-to-all | bytes 262144 | tf_op jit(solution)/shard_map/all_to_all | solution.py:524
  76.2 2.8 row_pass.2
  79.0 87.0 %all_to_all.48.refs_1_ = bf16[8,64,128]{2,1,0:T(8,128)(2,1)S(1)} all-to-all(bf16[8,64,128]{2,1,0:T(8,128)(2,1)S(1)} %get-tuple-element.149), channel_id=1, replica_groups=mesh['frames_0'=4,'frames_1'=8,'codes_0'=4,'codes_1'=2] {'codes_0','code..., dimensions={0} | all-to-all | bytes 262144 | tf_op jit(solution)/shard_map/all_to_all | solution.py:524
  166.1 4.5 %column_pass.4 = (f32[4,64,128]{2,1,0:T(8,128)S(1)}, f32[8,64,128]{2,1,0:T(8,128)S(1)}) custom-call(s32[8,64]{1,0:T(8,128)S(1)} %get-tuple-element.83.picks.refs_2_.refs_3_, f32[8,64,128]{2,1,0:T(8,128)S(1)} %all_to_all.45.refs_0_, bf16[8,64,128]{2,1,0:T(8,128)(2,1)S(1)} %all_to_all.48.refs_1_, f32[64,128]{1,0:T(8,128)S(1)} %get-tuple-element.142.refs_1_.refs_2_.refs_3_, ...), custom_call_target="tpu_custom_call" | custom-call | tf_op jit(solution)/shard_map/column_pass/pallas_call | solution.py:320
  170.5 9.7 %all_to_all.49.pieces_ref = f32[4,64,128]{2,1,0:T(8,128)S(1)} all-to-all(f32[4,64,128]{2,1,0:T(8,128)S(1)} %get-tuple-element.150), channel_id=1, replica_groups=mesh['frames_0'=4,'frames_1'=8,'codes_0'=4,'codes_1'=2] {'frames_0'}, dimensions={0} | all-to-all | bytes 262144 | tf_op jit(solution)/shard_map/all_to_all | solution.py:524
  180.2 12.4 %all_to_all.50.refs_1_ = bf16[8,64,128]{2,1,0:T(8,128)(2,1)S(1)} all-to-all(bf16[8,64,128]{2,1,0:T(8,128)(2,1)S(1)} %get-tuple-element.152), channel_id=1, replica_groups=mesh['frames_0'=4,'frames_1'=8,'codes_0'=4,'codes_1'=2] {'frames_1'}, dimensions={0} | all-to-all | bytes 262144 | tf_op jit(solution)/shard_map/all_to_all | solution.py:524
  192.6 2.8 row_pass.3
  195.4 89.8 %all_to_all.51.refs_1_ = bf16[8,64,128]{2,1,0:T(8,128)(2,1)S(1)} all-to-all(bf16[8,64,128]{2,1,0:T(8,128)(2,1)S(1)} %get-tuple-element.156), channel_id=1, replica_groups=mesh['frames_0'=4,'frames_1'=8,'codes_0'=4,'codes_1'=2] {'codes_0','code..., dimensions={0} | all-to-all | bytes 262144 | tf_op jit(solution)/shard_map/all_to_all | solution.py:524
  285.2 4.5 %column_pass.5 = (f32[4,64,128]{2,1,0:T(8,128)S(1)}, f32[64,128]{1,0:T(8,128)S(1)}) custom-call(s32[8,64]{1,0:T(8,128)S(1)} %get-tuple-element.83.picks.refs_2_.refs_3_, f32[8,64,128]{2,1,0:T(8,128)S(1)} %get-tuple-element.155.refs_0_, bf16[8,64,128]{2,1,0:T(8,128)(2,1)S(1)} %all_to_all.51.refs_1_, f32[64,128]{1,0:T(8,128)S(1)} %get-tuple-element.142.refs_1_.refs_2_.refs_3_, ...), custom_call_target="tpu_custom_call" | custom-call | tf_op jit(solution)/shard_map/column_pass/pallas_call | solution.py:320
  289.7 47.1 %all_to_all.52.pieces_ref = f32[4,64,128]{2,1,0:T(8,128)S(1)} all-to-all(f32[4,64,128]{2,1,0:T(8,128)S(1)} %get-tuple-element.157), channel_id=1, replica_groups=mesh['frames_0'=4,'frames_1'=8,'codes_0'=4,'codes_1'=2] {'frames_0'}, dimensions={0} | all-to-all | bytes 262144 | tf_op jit(solution)/shard_map/all_to_all | solution.py:524
  336.8 17.4 %all_to_all.53.change_ref = bf16[8,64,128]{2,1,0:T(8,128)(2,1)S(1)} all-to-all(bf16[8,64,128]{2,1,0:T(8,128)(2,1)S(1)} %combine.7), channel_id=1, replica_groups=mesh['frames_0'=4,'frames_1'=8,'codes_0'=4,'codes_1'=2] {'frames_1'}, dimensions={0} | all-to-all | bytes 262144 | tf_op jit(solution)/shard_map/all_to_all | solution.py:524
  354.3 0.7 finish.1
  (15 shorter events, 0.4 us)
Async XLA Ops:
  0.6 2.8 collective-permute-start.1
  0.7 10.1 %collective-permute-start = (bf16[1024,256]{1,0:T(8,128)(2,1)}, bf16[1024,256]{1,0:T(8,128)(2,1)S(1)}, u32[]{:S(2)}, u32[]{:S(2)}) collective-permute-start(bf16[1024,256]{1,0:T(8,128)(2,1)} %refs_0_.1), channel_id=1, source_target_pairs={{0,2},{1,7},{2,4},{3,1},{4,6},{5,3},{6,0},{7,5},{8,10},{9,15},{10,... | collective-permute-start | bytes 1572872 | tf_op jit(solution)/shard_map/ppermute | solution.py:479
  3.4 2.2 copy-start
  7.7 1.1 copy-start.1
  10.8 4.1 %collective-permute-start.4 = (bf16[1024,256]{1,0:T(8,128)(2,1)S(1)}, bf16[1024,256]{1,0:T(8,128)(2,1)S(1)}, u32[]{:S(2)}, u32[]{:S(2)}) collective-permute-start(bf16[1024,256]{1,0:T(8,128)(2,1)S(1)} %collective-permute-done.refs_0_), channel_id=1, source_target_pairs={{0,1},{1,0},{2,3},{3,2},{4,5},{5,4},{6,7},{7,6},{8,9},{9,8},{10,11... | collective-permute-start | bytes 1572872 | tf_op jit(solution)/shard_map/ppermute | solution.py:425
  10.9 9.3 %collective-permute-start.3 = (bf16[1024,256]{1,0:T(8,128)(2,1)S(1)}, bf16[1024,256]{1,0:T(8,128)(2,1)S(1)}, u32[]{:S(2)}, u32[]{:S(2)}) collective-permute-start(bf16[1024,256]{1,0:T(8,128)(2,1)S(1)} %copy-done.1), channel_id=1, source_target_pairs={{0,6},{1,3},{2,0},{3,5},{4,2},{5,7},{6,4},{7,1},{8,14},{9,11},{10,... | collective-permute-start | bytes 1572872 | tf_op jit(solution)/shard_map/ppermute | solution.py:505
  20.2 3.3 collective-permute-start.5
  20.2 9.2 %collective-permute-start.2 = (bf16[1024,256]{1,0:T(8,128)(2,1)S(1)}, bf16[1024,256]{1,0:T(8,128)(2,1)S(1)}, u32[]{:S(2)}, u32[]{:S(2)}) collective-permute-start(bf16[1024,256]{1,0:T(8,128)(2,1)S(1)} %collective-permute-done.refs_0_), channel_id=1, source_target_pairs={{0,2},{1,7},{2,4},{3,1},{4,6},{5,3},{6,0},{7,5},{8,10},{9,15},{10,... | collective-permute-start | bytes 1572872 | tf_op jit(solution)/shard_map/ppermute | solution.py:508
  29.4 2.1 collective-permute-start.6

commit v5 on v4

--- a/solution.py
+++ b/solution.py
@@ -46,10 +46,11 @@
                 (((1,), (1,)), ((), ())),
                 preferred_element_type=jnp.float32,
             )
-            logit_ref[b, s * BLK : (s + 3) * BLK, :] = three.astype(jnp.bfloat16)
-            part = jnp.max(three.reshape(3 * BLK // 8, 8, BLK), axis=0)
+            three = three.astype(jnp.bfloat16)
+            logit_ref[b, s * BLK : (s + 3) * BLK, :] = three
+            part = jnp.max(three.reshape(3 * BLK // 16, 16, BLK), axis=0)
             top = part if top is None else jnp.maximum(top, part)
-        high = jnp.max(top, axis=0, keepdims=True).astype(jnp.bfloat16).astype(jnp.float32)
+        high = jnp.max(top.astype(jnp.float32), axis=0, keepdims=True)
         total = None
         for s in range(CAP):
             tile = logit_ref[b, s * BLK : (s + 1) * BLK, :].astype(jnp.float32)
@@ -503,12 +504,12 @@
     made = use(made, "own", 1, swap(frames))
     late, made = lax.optimization_barrier((frames, made))
     back = lax.ppermute(late, CODES, crossing(-1))
-    made = use(made, "own", 0, frames)
     near, made = lax.optimization_barrier((near, made))
     far = lax.ppermute(near, CODES, crossing(1))
     other = swap(near)
     made = use(made, "near", 0, near)
     made = use(made, "near", 1, other)
+    made = use(made, "own", 0, frames)
     back, made = lax.optimization_barrier((back, made))
     other = swap(back)
     made = use(made, "back", 0, back)

time: 357 us -> 357 us (level)
  transfers between devices with their start and end apart: 7 -> 7, of which waited for: 2 -> 3; matrix products, arithmetic and copies ran while one was open for 0% -> 0% of each run, Pallas kernels for 4% -> 4%
where the time goes in v5:
time: 357 us; the launch traced here: 355 us
  blocking collectives  302 us (85%)
  Pallas kernels  35 us (10%)
  waiting for transfers between devices  9.06 us (3%)
  starting transfers between devices  4.91 us (1%)
    all_to_all x9, blocking collectives, exchange(): return lax.all_to_all(pieces, axes, 0, 0, tiled=True)  302 us
    pallas_call x8, Pallas kernels, make_tiles(): pl.pallas_call(functools.partial(tiles_kernel, parts), grid_spec=pltpu.Pr...  14.9 us
    pallas_call x3, Pallas kernels, column_pass(): pl.pallas_call(functools.partial(column_kernel, len(pieces), last), grid_...  13.4 us
  transfers between devices with their start and end apart: 7, of which 3 were waited for; matrix products, arithmetic and copies ran while one was open for 0% of the time, Pallas kernels for 4%

profile of v5, /device:TPU:34, one launch (start us, length us, event | category | flops | bytes accessed | tf_op | source)
XLA Modules:
  0.0 354.7 jit_solution(16676399593568160508)
XLA Ops:
  0.7 1.6 collective-permute-start
  2.3 0.8 copy.33.pattern_ref
  3.1 0.3 tables.1
  3.4 2.2 copy-done
  5.6 1.9 make_tiles.8
  7.4 2.8 collective-permute-done.refs_0_
  10.2 1.7 collective-permute-start.3
  11.9 1.9 make_tiles.9
  13.8 1.9 make_tiles.10
  15.7 1.9 make_tiles.11
  17.6 2.0 collective-permute-done.3.refs_0_
  19.6 1.5 collective-permute-start.2
  21.1 1.9 make_tiles.12
  23.0 1.9 make_tiles.13
  24.8 4.2 %collective-permute-done.2.refs_0_ = bf16[1024,256]{1,0:T(8,128)(2,1)S(1)} collective-permute-done((bf16[1024,256]{1,0:T(8,128)(2,1)S(1)}, bf16[1024,256]{1,0:T(8,128)(2,1)S(1)}, u32[]{:S(2)}, u32[]{:S(2)}) %collective-permute-start.2) | collective-permute-done | bytes 524320 | tf_op jit(solution)/shard_map/ppermute | solution.py:508
  29.1 1.9 make_tiles.14
  31.0 1.9 make_tiles.15
  32.9 12.3 %all_to_all.45.refs_0_ = f32[8,64,128]{2,1,0:T(8,128)S(1)} all-to-all(f32[8,64,128]{2,1,0:T(8,128)S(1)} %get-tuple-element.141), channel_id=1, replica_groups=mesh['frames_0'=4,'frames_1'=8,'codes_0'=4,'codes_1'=2] {'codes_0','code..., dimensions={0} | all-to-all | bytes 524288 | tf_op jit(solution)/shard_map/all_to_all | solution.py:525
  45.2 4.4 %column_pass.3 = f32[4,64,128]{2,1,0:T(8,128)S(1)} custom-call(s32[8,64]{1,0:T(8,128)S(1)} %get-tuple-element.83.picks.refs_2_.refs_3_, f32[8,64,128]{2,1,0:T(8,128)S(1)} %all_to_all.45.refs_0_, f32[64,128]{1,0:T(8,128)S(1)} %get-tuple-element.142.refs_1_.refs_2_.refs_3_, s32[8,64]{1,0:T(8,128)S(1)} %get-tuple-element.83.picks.refs_2_.refs_3_, ...), custom_call_target="tpu_custom_call" | custom-call | tf_op jit(solution)/shard_map/column_pass/pallas_call | solution.py:321
  49.7 10.2 %all_to_all.46.pieces_ref = f32[4,64,128]{2,1,0:T(8,128)S(1)} all-to-all(f32[4,64,128]{2,1,0:T(8,128)S(1)} %column_pass.3), channel_id=1, replica_groups=mesh['frames_0'=4,'frames_1'=8,'codes_0'=4,'codes_1'=2] {'frames_0'}, dimensions={0} | all-to-all | bytes 262144 | tf_op jit(solution)/shard_map/all_to_all | solution.py:525
  60.0 16.0 %all_to_all.47.refs_0_ = bf16[8,64,128]{2,1,0:T(8,128)(2,1)S(1)} all-to-all(bf16[8,64,128]{2,1,0:T(8,128)(2,1)S(1)} %get-tuple-element.145), channel_id=1, replica_groups=mesh['frames_0'=4,'frames_1'=8,'codes_0'=4,'codes_1'=2] {'frames_1'}, dimensions={0} | all-to-all | bytes 262144 | tf_op jit(solution)/shard_map/all_to_all | solution.py:525
  75.9 2.8 row_pass.2
  78.7 87.0 %all_to_all.48.refs_1_ = bf16[8,64,128]{2,1,0:T(8,128)(2,1)S(1)} all-to-all(bf16[8,64,128]{2,1,0:T(8,128)(2,1)S(1)} %get-tuple-element.149), channel_id=1, replica_groups=mesh['frames_0'=4,'frames_1'=8,'codes_0'=4,'codes_1'=2] {'codes_0','code..., dimensions={0} | all-to-all | bytes 262144 | tf_op jit(solution)/shard_map/all_to_all | solution.py:525
  165.8 4.5 %column_pass.4 = (f32[4,64,128]{2,1,0:T(8,128)S(1)}, f32[8,64,128]{2,1,0:T(8,128)S(1)}) custom-call(s32[8,64]{1,0:T(8,128)S(1)} %get-tuple-element.83.picks.refs_2_.refs_3_, f32[8,64,128]{2,1,0:T(8,128)S(1)} %all_to_all.45.refs_0_, bf16[8,64,128]{2,1,0:T(8,128)(2,1)S(1)} %all_to_all.48.refs_1_, f32[64,128]{1,0:T(8,128)S(1)} %get-tuple-element.142.refs_1_.refs_2_.refs_3_, ...), custom_call_target="tpu_custom_call" | custom-call | tf_op jit(solution)/shard_map/column_pass/pallas_call | solution.py:321
  170.3 9.7 %all_to_all.49.pieces_ref = f32[4,64,128]{2,1,0:T(8,128)S(1)} all-to-all(f32[4,64,128]{2,1,0:T(8,128)S(1)} %get-tuple-element.150), channel_id=1, replica_groups=mesh['frames_0'=4,'frames_1'=8,'codes_0'=4,'codes_1'=2] {'frames_0'}, dimensions={0} | all-to-all | bytes 262144 | tf_op jit(solution)/shard_map/all_to_all | solution.py:525
  180.0 12.4 %all_to_all.50.refs_1_ = bf16[8,64,128]{2,1,0:T(8,128)(2,1)S(1)} all-to-all(bf16[8,64,128]{2,1,0:T(8,128)(2,1)S(1)} %get-tuple-element.152), channel_id=1, replica_groups=mesh['frames_0'=4,'frames_1'=8,'codes_0'=4,'codes_1'=2] {'frames_1'}, dimensions={0} | all-to-all | bytes 262144 | tf_op jit(solution)/shard_map/all_to_all | solution.py:525
  192.4 2.8 row_pass.3
  195.2 89.8 %all_to_all.51.refs_1_ = bf16[8,64,128]{2,1,0:T(8,128)(2,1)S(1)} all-to-all(bf16[8,64,128]{2,1,0:T(8,128)(2,1)S(1)} %get-tuple-element.156), channel_id=1, replica_groups=mesh['frames_0'=4,'frames_1'=8,'codes_0'=4,'codes_1'=2] {'codes_0','code..., dimensions={0} | all-to-all | bytes 262144 | tf_op jit(solution)/shard_map/all_to_all | solution.py:525
  284.9 4.5 %column_pass.5 = (f32[4,64,128]{2,1,0:T(8,128)S(1)}, f32[64,128]{1,0:T(8,128)S(1)}) custom-call(s32[8,64]{1,0:T(8,128)S(1)} %get-tuple-element.83.picks.refs_2_.refs_3_, f32[8,64,128]{2,1,0:T(8,128)S(1)} %get-tuple-element.155.refs_0_, bf16[8,64,128]{2,1,0:T(8,128)(2,1)S(1)} %all_to_all.51.refs_1_, f32[64,128]{1,0:T(8,128)S(1)} %get-tuple-element.142.refs_1_.refs_2_.refs_3_, ...), custom_call_target="tpu_custom_call" | custom-call | tf_op jit(solution)/shard_map/column_pass/pallas_call | solution.py:321
  289.4 47.1 %all_to_all.52.pieces_ref = f32[4,64,128]{2,1,0:T(8,128)S(1)} all-to-all(f32[4,64,128]{2,1,0:T(8,128)S(1)} %get-tuple-element.157), channel_id=1, replica_groups=mesh['frames_0'=4,'frames_1'=8,'codes_0'=4,'codes_1'=2] {'frames_0'}, dimensions={0} | all-to-all | bytes 262144 | tf_op jit(solution)/shard_map/all_to_all | solution.py:525
  336.6 17.4 %all_to_all.53.change_ref = bf16[8,64,128]{2,1,0:T(8,128)(2,1)S(1)} all-to-all(bf16[8,64,128]{2,1,0:T(8,128)(2,1)S(1)} %combine.7), channel_id=1, replica_groups=mesh['frames_0'=4,'frames_1'=8,'codes_0'=4,'codes_1'=2] {'frames_1'}, dimensions={0} | all-to-all | bytes 262144 | tf_op jit(solution)/shard_map/all_to_all | solution.py:525
  354.0 0.7 finish.1
  (15 shorter events, 0.3 us)
Async XLA Ops:
  0.6 2.8 collective-permute-start.1
  0.7 9.5 %collective-permute-start = (bf16[1024,256]{1,0:T(8,128)(2,1)}, bf16[1024,256]{1,0:T(8,128)(2,1)S(1)}, u32[]{:S(2)}, u32[]{:S(2)}) collective-permute-start(bf16[1024,256]{1,0:T(8,128)(2,1)} %refs_0_.1), channel_id=1, source_target_pairs={{0,2},{1,7},{2,4},{3,1},{4,6},{5,3},{6,0},{7,5},{8,10},{9,15},{10,... | collective-permute-start | bytes 1572872 | tf_op jit(solution)/shard_map/ppermute | solution.py:480
  3.4 2.2 copy-start
  10.2 3.6 %collective-permute-start.4 = (bf16[1024,256]{1,0:T(8,128)(2,1)S(1)}, bf16[1024,256]{1,0:T(8,128)(2,1)S(1)}, u32[]{:S(2)}, u32[]{:S(2)}) collective-permute-start(bf16[1024,256]{1,0:T(8,128)(2,1)S(1)} %collective-permute-done.refs_0_), channel_id=1, source_target_pairs={{0,1},{1,0},{2,3},{3,2},{4,5},{5,4},{6,7},{7,6},{8,9},{9,8},{10,11... | collective-permute-start | bytes 1572872 | tf_op jit(solution)/shard_map/ppermute | solution.py:426
  10.2 9.4 %collective-permute-start.3 = (bf16[1024,256]{1,0:T(8,128)(2,1)}, bf16[1024,256]{1,0:T(8,128)(2,1)S(1)}, u32[]{:S(2)}, u32[]{:S(2)}) collective-permute-start(bf16[1024,256]{1,0:T(8,128)(2,1)} %refs_0_.1), channel_id=1, source_target_pairs={{0,6},{1,3},{2,0},{3,5},{4,2},{5,7},{6,4},{7,1},{8,14},{9,11},{10,... | collective-permute-start | bytes 1572872 | tf_op jit(solution)/shard_map/ppermute | solution.py:506
  13.8 1.9 copy-start.1
  19.6 3.4 collective-permute-start.5
  19.6 9.5 %collective-permute-start.2 = (bf16[1024,256]{1,0:T(8,128)(2,1)S(1)}, bf16[1024,256]{1,0:T(8,128)(2,1)S(1)}, u32[]{:S(2)}, u32[]{:S(2)}) collective-permute-start(bf16[1024,256]{1,0:T(8,128)(2,1)S(1)} %collective-permute-done.refs_0_), channel_id=1, source_target_pairs={{0,2},{1,7},{2,4},{3,1},{4,6},{5,3},{6,0},{7,5},{8,10},{9,15},{10,... | collective-permute-start | bytes 1572872 | tf_op jit(solution)/shard_map/ppermute | solution.py:508
  29.1 1.9 collective-permute-start.6
